TPU v7x, 512 devices: a whole 4x8x8 slice. The times are simulated.
512 devices in a mesh: pipe: 16 (over y, x_hi), expert: 32 (over z, x_lo, core).
Axes of the slice: x: 4 (x_hi: 2, x_lo: 2; x = x_hi * 2 + x_lo), y: 8, z: 8, core: 2. Of those that a mesh axis runs over, the one named last changes fastest.
Arguments:
- section_acts: bfloat16 [16, 2048, 2560], P('pipe', 'expert'), may hold values from -6 to 6
- section_grads: bfloat16 [16, 2048, 2560], P('pipe', 'expert'), may hold values from -6 to 6
- routes_fwd: int32 [16, 2048, 2], P('pipe', 'expert'), may hold values from 0 to 7, all different within a row; in each aligned block of 64 rows (0 to 63, 64 to 127, ..., all dimensions but the last counted through in order) at most 20 rows name the same one
- gate_fwd: int32 [16, 2048, 2], P('pipe', 'expert'), may hold values from 32 to 255
- routes_bwd: int32 [16, 2048, 2], P('pipe', 'expert'), may hold values from 0 to 7, all different within a row; in each aligned block of 64 rows (0 to 63, 64 to 127, ..., all dimensions but the last counted through in order) at most 20 rows name the same one
- gate_bwd: int32 [16, 2048, 2], P('pipe', 'expert'), may hold values from 32 to 255
- saved_pre: bfloat16 [16, 32, 32, 20, 384], P('pipe', 'expert'), may hold values from -6 to 6
- w_gate_up: bfloat16 [16, 32, 2560, 384], P('pipe', 'expert'), may hold values from -0.125 to 0.125
- w_down: bfloat16 [16, 32, 192, 2560], P('pipe', 'expert'), may hold values from -0.21875 to 0.21875
Outputs:
- moe_out: bfloat16 [16, 2048, 2560], P('pipe', 'expert')
- input_grad: bfloat16 [16, 2048, 2560], P('pipe', 'expert')
Inputs may be any that keep to these rules, and one draw needn't show every extreme that they name: `routes_fwd`: among the tokens of one index of expert, no expert is named more than 20 times; in every draw some expert is named exactly 20 times by the tokens of some index. The 2 experts of a token differ. `routes_bwd`: among the tokens of one index of expert, no expert is named more than 20 times; in every draw some expert is named exactly 20 times by the tokens of some index. The 2 experts of a token differ.
All inputs are finite; a program needn't handle non-finite values.
Results may differ from a plain program's by a relative error of at most 0.0059.
Values may be sent and summed in bfloat16 or wider, within the bound.
A program may use at most 128 MiB of HBM per device.

v0:
```python
import jax
import jax.numpy as jnp
from jax import lax
from jax.sharding import PartitionSpec as P

EXPERTS = 8


def from_behind(array, axis, by):
    devices = lax.axis_size(axis)
    return lax.ppermute(array, axis, [(i, (i + by) % devices) for i in range(devices)])


def slot_rows(routes, capacity):
    assigned = routes.reshape(-1)
    onehot = (assigned[:, None] == jnp.arange(EXPERTS, dtype=jnp.int32)[None, :]).astype(jnp.int32)
    earlier = jnp.cumsum(onehot, axis=0) - onehot
    return assigned * capacity + jnp.sum(earlier * onehot, axis=1)


def pack_rows(values, flat_rows, capacity, per_token):
    selector = (
        jnp.arange(EXPERTS * capacity, dtype=jnp.int32)[:, None] == flat_rows[None, :]
    ).astype(jnp.bfloat16)
    repeated = jnp.repeat(values, per_token, axis=0)
    packed = jnp.dot(selector, repeated, preferred_element_type=jnp.float32).astype(jnp.bfloat16)
    return packed.reshape(EXPERTS, capacity, values.shape[1])


def combine_rows(residual_in, outputs, flat_rows, gate_ints):
    token_count, per_token = gate_ints.shape
    picked = (
        jnp.take(outputs, flat_rows, axis=0)
        .reshape(token_count, per_token, outputs.shape[1])
        .astype(jnp.float32)
    )
    weights = gate_ints.astype(jnp.float32) / 128.0
    return (residual_in.astype(jnp.float32) + jnp.sum(picked * weights[..., None], axis=1)).astype(
        jnp.bfloat16
    )


def expert_work(rows_in, rows_grad, inner_w, outer_w, saved_acts):
    hidden_units = outer_w.shape[0]
    projected = jnp.dot(rows_in, inner_w, preferred_element_type=jnp.float32)
    hidden_act = (jax.nn.silu(projected[:, :hidden_units]) * projected[:, hidden_units:]).astype(
        jnp.bfloat16
    )
    fwd_part = jnp.dot(hidden_act, outer_w, preferred_element_type=jnp.float32).astype(jnp.bfloat16)
    gate_saved = saved_acts[:, :hidden_units].astype(jnp.float32)
    up_saved = saved_acts[:, hidden_units:].astype(jnp.float32)
    back_hidden = lax.dot_general(
        rows_grad, outer_w, (((1,), (1,)), ((), ())), preferred_element_type=jnp.float32
    )
    sigmoid_gate = jax.nn.sigmoid(gate_saved)
    back_pre = jnp.concatenate(
        [
            back_hidden * up_saved * sigmoid_gate * (1.0 + gate_saved * (1.0 - sigmoid_gate)),
            back_hidden * gate_saved * sigmoid_gate,
        ],
        axis=-1,
    ).astype(jnp.bfloat16)
    back_part = lax.dot_general(
        back_pre, inner_w, (((1,), (1,)), ((), ())), preferred_element_type=jnp.float32
    ).astype(jnp.bfloat16)
    return (fwd_part, back_part)


def on_device(
    section_acts,
    section_grads,
    routes_fwd,
    gate_fwd,
    routes_bwd,
    gate_bwd,
    saved_pre,
    w_gate_up,
    w_down,
):
    section_in = from_behind(section_acts, "pipe", 1)[0]
    grad_in = from_behind(section_grads, "pipe", -1)[0]
    blocks = lax.axis_size("expert")
    group = blocks // EXPERTS
    capacity = saved_pre.shape[3]
    model_width = section_in.shape[1]
    per_token = routes_fwd.shape[2]
    inner_w = w_gate_up[0, 0]
    outer_w = w_down[0, 0]
    saved_acts = saved_pre[0, 0].reshape(blocks * capacity, saved_pre.shape[4])
    rows_fwd = slot_rows(routes_fwd[0], capacity)
    rows_bwd = slot_rows(routes_bwd[0], capacity)
    packed_in = pack_rows(section_in, rows_fwd, capacity, per_token)
    packed_grad = pack_rows(grad_in, rows_bwd, capacity, per_token)
    sent_in = jnp.repeat(packed_in, group, axis=0)
    sent_grad = jnp.repeat(packed_grad, group, axis=0)
    got_in, got_grad = (
        lax.all_to_all(sent_in, "expert", split_axis=0, concat_axis=0, tiled=True),
        lax.all_to_all(sent_grad, "expert", split_axis=0, concat_axis=0, tiled=True),
    )
    fwd_part, back_part = expert_work(
        got_in.reshape(blocks * capacity, model_width),
        got_grad.reshape(blocks * capacity, model_width),
        inner_w,
        outer_w,
        saved_acts,
    )
    ret_fwd, ret_bwd = (
        lax.all_to_all(
            fwd_part.reshape(blocks, capacity, model_width),
            "expert",
            split_axis=0,
            concat_axis=0,
            tiled=True,
        ),
        lax.all_to_all(
            back_part.reshape(blocks, capacity, model_width),
            "expert",
            split_axis=0,
            concat_axis=0,
            tiled=True,
        ),
    )
    fwd_out = jnp.sum(
        ret_fwd.reshape(EXPERTS, group, capacity, model_width), axis=1, dtype=jnp.float32
    )
    back_out = jnp.sum(
        ret_bwd.reshape(EXPERTS, group, capacity, model_width), axis=1, dtype=jnp.float32
    )
    fwd_out = fwd_out.astype(jnp.bfloat16).reshape(EXPERTS * capacity, model_width)
    back_out = back_out.astype(jnp.bfloat16).reshape(EXPERTS * capacity, model_width)
    moe_out = combine_rows(section_in, fwd_out, rows_fwd, gate_fwd[0])
    input_grad = combine_rows(grad_in, back_out, rows_bwd, gate_bwd[0])
    return (moe_out[None], input_grad[None])


def solution(mesh):
    placed = (
        P("pipe", "expert", None),
        P("pipe", "expert", None),
        P("pipe", "expert", None),
        P("pipe", "expert", None),
        P("pipe", "expert", None),
        P("pipe", "expert", None),
        P("pipe", "expert", None, None, None),
        P("pipe", "expert", None, None),
        P("pipe", "expert", None, None),
    )
    return jax.shard_map(
        on_device,
        mesh=mesh,
        in_specs=placed,
        out_specs=(P("pipe", "expert", None), P("pipe", "expert", None)),
        check_vma=False,
    )
```

profile of v0, /device:TPU:1, one launch (start us, length us, event | category | flops | bytes accessed | tf_op | source)
XLA Modules:
  0.0 430.2 jit_solution(7083068082732890859)
XLA Ops:
  0.6 8.5 %collective-permute-start.1 = (bf16[1,64,2560]{2,1,0:T(8,128)(2,1)}, bf16[1,64,2560]{2,1,0:T(8,128)(2,1)S(1)}, u32[]{:S(2)}, u32[]{:S(2)}) collective-permute-start(bf16[1,64,2560]{2,1,0:T(8,128)(2,1)} %param.12), channel_id=1, source_target_pairs={{0,480},{32,0},{64,32},{96,64},{128,96},{160,128},{192,160},{224,1... | collective-permute-start | bytes 983048 | tf_op jit(solution)/shard_map/ppermute | solution.py:11
  10.5 5.3 %collective-permute-done.1 = bf16[1,64,2560]{2,1,0:T(8,128)(2,1)S(1)} collective-permute-done((bf16[1,64,2560]{2,1,0:T(8,128)(2,1)}, bf16[1,64,2560]{2,1,0:T(8,128)(2,1)S(1)}, u32[]{:S(2)}, u32[]{:S(2)}) %collective-permute-start.1) | collective-permute-done | bytes 327712 | tf_op jit(solution)/shard_map/ppermute | solution.py:11
  21.9 12.2 %all-to-all-start.2 = ((bf16[32,20,2560]{2,1,0:T(8,128)(2,1)}), bf16[32,20,2560]{2,1,0:T(8,128)(2,1)}, u32[]{:S(2)}, u32[]{:S(2)}) async-start(bf16[32,20,2560]{2,1,0:T(8,128)(2,1)} %bitcast.36), calls=%async_computation.2 | async-start | bytes 7864320 | tf_op jit(solution)/shard_map/all_to_all | solution.py:98
  34.1 4.1 collective-permute-start
  38.9 21.7 %collective-permute-done = bf16[1,64,2560]{2,1,0:T(8,128)(2,1)S(1)} collective-permute-done((bf16[1,64,2560]{2,1,0:T(8,128)(2,1)S(1)}, bf16[1,64,2560]{2,1,0:T(8,128)(2,1)S(1)}, u32[]{:S(2)}, u32[]{:S(2)}) %collective-permute-start) | collective-permute-done | bytes 327712 | tf_op jit(solution)/shard_map/ppermute | solution.py:11
  64.6 60.5 %all-to-all-done.2 = bf16[32,20,2560]{2,1,0:T(8,128)(2,1)} async-done(((bf16[32,20,2560]{2,1,0:T(8,128)(2,1)}), bf16[32,20,2560]{2,1,0:T(8,128)(2,1)}, u32[]{:S(2)}, u32[]{:S(2)}) %all-to-all-start.2) | async-done | bytes 3276832 | tf_op jit(solution)/shard_map/all_to_all | solution.py:98
  127.4 5.0 %all-to-all-start = ((bf16[32,20,2560]{2,1,0:T(8,128)(2,1)}), bf16[32,20,2560]{2,1,0:T(8,128)(2,1)}, u32[]{:S(2)}, u32[]{:S(2)}) async-start(bf16[32,20,2560]{2,1,0:T(8,128)(2,1)} %bitcast.37), calls=%async_computation | async-start | bytes 7864320 | tf_op jit(solution)/shard_map/all_to_all | solution.py:97
  133.2 5.6 %reshape.105 = bf16[640,2560]{1,0:T(8,128)(2,1)} reshape(bf16[32,20,2560]{2,1,0:T(8,128)(2,1)} %all-to-all-done.2) | data formatting | bytes 6553600 | tf_op jit(solution)/shard_map/reshape | solution.py:102
  138.8 3.4 fusion.13
  142.3 3.7 convolution_convert_fusion
  146.0 5.5 %reshape.106 = bf16[32,20,2560]{2,1,0:T(8,128)(2,1)} reshape(bf16[640,2560]{1,0:T(8,128)(2,1)} %convolution_convert_fusion) | data formatting | bytes 6553600 | tf_op jit(solution)/shard_map/reshape | solution.py:116
  151.5 72.0 %all-to-all-done = bf16[32,20,2560]{2,1,0:T(8,128)(2,1)} async-done(((bf16[32,20,2560]{2,1,0:T(8,128)(2,1)}), bf16[32,20,2560]{2,1,0:T(8,128)(2,1)}, u32[]{:S(2)}, u32[]{:S(2)}) %all-to-all-start) | async-done | bytes 3276832 | tf_op jit(solution)/shard_map/all_to_all | solution.py:97
  223.5 4.9 %all-to-all-start.3 = ((bf16[32,20,2560]{2,1,0:T(8,128)(2,1)}), bf16[32,20,2560]{2,1,0:T(8,128)(2,1)}, u32[]{:S(2)}, u32[]{:S(2)}) async-start(bf16[32,20,2560]{2,1,0:T(8,128)(2,1)} %reshape.106), calls=%async_computation.3 | async-start | bytes 7864320 | tf_op jit(solution)/shard_map/all_to_all | solution.py:115
  228.4 5.6 %reshape.98 = bf16[640,2560]{1,0:T(8,128)(2,1)} reshape(bf16[32,20,2560]{2,1,0:T(8,128)(2,1)} %all-to-all-done) | data formatting | bytes 6553600 | tf_op jit(solution)/shard_map/reshape | solution.py:101
  234.0 3.7 fusion.1
  237.7 2.9 convolution_convert_fusion.1
  240.6 5.5 %reshape.99 = bf16[32,20,2560]{2,1,0:T(8,128)(2,1)} reshape(bf16[640,2560]{1,0:T(8,128)(2,1)} %convolution_convert_fusion.1) | data formatting | bytes 6553600 | tf_op jit(solution)/shard_map/reshape | solution.py:109
  246.1 73.4 %all-to-all-done.3 = bf16[32,20,2560]{2,1,0:T(8,128)(2,1)} async-done(((bf16[32,20,2560]{2,1,0:T(8,128)(2,1)}), bf16[32,20,2560]{2,1,0:T(8,128)(2,1)}, u32[]{:S(2)}, u32[]{:S(2)}) %all-to-all-start.3) | async-done | bytes 3276832 | tf_op jit(solution)/shard_map/all_to_all | solution.py:115
  319.4 4.9 %all-to-all-start.1 = ((bf16[32,20,2560]{2,1,0:T(8,128)(2,1)}), bf16[32,20,2560]{2,1,0:T(8,128)(2,1)}, u32[]{:S(2)}, u32[]{:S(2)}) async-start(bf16[32,20,2560]{2,1,0:T(8,128)(2,1)} %reshape.99), calls=%async_computation.1 | async-start | bytes 7864320 | tf_op jit(solution)/shard_map/all_to_all | solution.py:108
  324.6 2.7 bitcast_reduce_fusion
  329.4 85.9 %all-to-all-done.1 = bf16[32,20,2560]{2,1,0:T(8,128)(2,1)} async-done(((bf16[32,20,2560]{2,1,0:T(8,128)(2,1)}), bf16[32,20,2560]{2,1,0:T(8,128)(2,1)}, u32[]{:S(2)}, u32[]{:S(2)}) %all-to-all-start.1) | async-done | bytes 3276832 | tf_op jit(solution)/shard_map/all_to_all | solution.py:108
  415.4 2.7 bitcast_reduce_fusion.1
  420.5 3.1 reshape.109
  425.4 3.2 multiply_reduce_fusion.1
  (69 shorter events, 23.1 us)
Async XLA Ops:
  0.6 141.6 %copy-start = (bf16[1,1,2560,384]{3,2,1,0:T(8,128)(2,1)S(1)}, bf16[1,1,2560,384]{3,2,1,0:T(8,128)(2,1)}, u32[]{:S(2)}) copy-start(bf16[1,1,2560,384]{3,2,1,0:T(8,128)(2,1)} %param.18) | copy-start | bytes 5898244
  0.6 15.2 %collective-permute-start.1 = (bf16[1,64,2560]{2,1,0:T(8,128)(2,1)}, bf16[1,64,2560]{2,1,0:T(8,128)(2,1)S(1)}, u32[]{:S(2)}, u32[]{:S(2)}) collective-permute-start(bf16[1,64,2560]{2,1,0:T(8,128)(2,1)} %param.12), channel_id=1, source_target_pairs={{0,480},{32,0},{64,32},{96,64},{128,96},{160,128},{192,160},{224,1... | collective-permute-start | bytes 983048 | tf_op jit(solution)/shard_map/ppermute | solution.py:11
  15.8 0.7 copy-start.2
  21.9 12.2 %copy-start.11 = (bf16[1,64,2560]{2,1,0:T(8,128)(2,1)S(1)}, bf16[1,64,2560]{2,1,0:T(8,128)(2,1)}, u32[]{:S(2)}) copy-start(bf16[1,64,2560]{2,1,0:T(8,128)(2,1)} %param.11) | copy-start | bytes 983044
  21.9 16.4 %copy-start.7 = (s32[1,64,2]{1,2,0:T(2,128)S(1)}, s32[1,64,2]{1,2,0:T(2,128)}, u32[]{:S(2)}) copy-start(s32[1,64,2]{1,2,0:T(2,128)} %param.13) | copy-start | bytes 1540
  21.9 103.2 %all-to-all-start.2 = ((bf16[32,20,2560]{2,1,0:T(8,128)(2,1)}), bf16[32,20,2560]{2,1,0:T(8,128)(2,1)}, u32[]{:S(2)}, u32[]{:S(2)}) async-start(bf16[32,20,2560]{2,1,0:T(8,128)(2,1)} %bitcast.36), calls=%async_computation.2 | async-start | bytes 7864320 | tf_op jit(solution)/shard_map/all_to_all | solution.py:98
  34.1 26.5 %collective-permute-start = (bf16[1,64,2560]{2,1,0:T(8,128)(2,1)S(1)}, bf16[1,64,2560]{2,1,0:T(8,128)(2,1)S(1)}, u32[]{:S(2)}, u32[]{:S(2)}) collective-permute-start(bf16[1,64,2560]{2,1,0:T(8,128)(2,1)S(1)} %copy-done.11), channel_id=1, source_target_pairs={{0,32},{32,64},{64,96},{96,128},{128,160},{160,192},{192,224},{224... | collective-permute-start | bytes 983048 | tf_op jit(solution)/shard_map/ppermute | solution.py:11
  60.6 0.7 copy-start.4
  127.4 5.0 %copy-start.6 = (bf16[1,1,32,20,384]{4,2,3,1,0:T(8,128)(2,1)S(1)}, bf16[1,1,32,20,384]{4,2,3,1,0:T(8,128)(2,1)}, u32[]{:S(2)}) copy-start(bf16[1,1,32,20,384]{4,2,3,1,0:T(8,128)(2,1)} %param.17) | copy-start | bytes 1474564
  127.4 96.1 %all-to-all-start = ((bf16[32,20,2560]{2,1,0:T(8,128)(2,1)}), bf16[32,20,2560]{2,1,0:T(8,128)(2,1)}, u32[]{:S(2)}, u32[]{:S(2)}) async-start(bf16[32,20,2560]{2,1,0:T(8,128)(2,1)} %bitcast.37), calls=%async_computation | async-start | bytes 7864320 | tf_op jit(solution)/shard_map/all_to_all | solution.py:97
  223.5 96.0 %all-to-all-start.3 = ((bf16[32,20,2560]{2,1,0:T(8,128)(2,1)}), bf16[32,20,2560]{2,1,0:T(8,128)(2,1)}, u32[]{:S(2)}, u32[]{:S(2)}) async-start(bf16[32,20,2560]{2,1,0:T(8,128)(2,1)} %reshape.106), calls=%async_computation.3 | async-start | bytes 7864320 | tf_op jit(solution)/shard_map/all_to_all | solution.py:115
  234.0 3.7 copy-start.10
  246.1 78.3 %copy-start.8 = (s32[1,64,2]{1,2,0:T(2,128)S(1)}, s32[1,64,2]{1,2,0:T(2,128)}, u32[]{:S(2)}) copy-start(s32[1,64,2]{1,2,0:T(2,128)} %param.16) | copy-start | bytes 1540
  246.1 78.4 %copy-start.9 = (s32[1,64,2]{1,2,0:T(2,128)S(1)}, s32[1,64,2]{1,2,0:T(2,128)}, u32[]{:S(2)}) copy-start(s32[1,64,2]{1,2,0:T(2,128)} %param.14) | copy-start | bytes 1540
  319.4 96.0 %all-to-all-start.1 = ((bf16[32,20,2560]{2,1,0:T(8,128)(2,1)}), bf16[32,20,2560]{2,1,0:T(8,128)(2,1)}, u32[]{:S(2)}, u32[]{:S(2)}) async-start(bf16[32,20,2560]{2,1,0:T(8,128)(2,1)} %reshape.99), calls=%async_computation.1 | async-start | bytes 7864320 | tf_op jit(solution)/shard_map/all_to_all | solution.py:108
  420.5 9.7 %copy-start.1 = (bf16[1,1,2560,384]{3,2,1,0:T(8,128)(2,1)S(1)}, bf16[1,1,2560,384]{3,2,1,0:T(8,128)(2,1)}, u32[]{:S(2)}) copy-start(bf16[1,1,2560,384]{3,2,1,0:T(8,128)(2,1)} %param.18) | copy-start | bytes 5898244
  423.6 5.0 %copy-start.3 = (bf16[1,64,2560]{2,1,0:T(8,128)(2,1)S(1)}, bf16[1,64,2560]{2,1,0:T(8,128)(2,1)}, u32[]{:S(2)}) copy-start(bf16[1,64,2560]{2,1,0:T(8,128)(2,1)} %copy-done.2) | copy-start | bytes 983044
  423.6 5.8 %copy-start.5 = (bf16[1,64,2560]{2,1,0:T(8,128)(2,1)S(1)}, bf16[1,64,2560]{2,1,0:T(8,128)(2,1)}, u32[]{:S(2)}) copy-start(bf16[1,64,2560]{2,1,0:T(8,128)(2,1)} %copy-done.4) | copy-start | bytes 983044
where the time goes:
time: 431 us; the launch traced here: 430 us
  waiting for transfers between devices  319 us (74%)
  local copies, waits for them, and re-layouts  40.2 us (9%)
  starting transfers between devices  39.7 us (9%)
  matrix products  16.3 us (4%)
  other arithmetic  14.3 us (3%)
    all_to_all x1, waiting for transfers between devices, on_device(): lax.all_to_all(fwd_part.reshape(blocks, capacity, model_width), 'expert',...  85.9 us
    all_to_all x1, waiting for transfers between devices, on_device(): lax.all_to_all(back_part.reshape(blocks, capacity, model_width), 'expert'...  73.4 us
    all_to_all x1, waiting for transfers between devices, on_device(): lax.all_to_all(sent_in, 'expert', split_axis=0, concat_axis=0, tiled=True)  72 us
    all_to_all x1, waiting for transfers between devices, on_device(): lax.all_to_all(sent_grad, 'expert', split_axis=0, concat_axis=0, tiled=True)  60.5 us
    ppermute x2, waiting for transfers between devices, from_behind(): lax.ppermute(array, axis, [(i, (i + by) % devices) for i in range(devices)])  27 us
    ppermute x2, starting transfers between devices, from_behind(): lax.ppermute(array, axis, [(i, (i + by) % devices) for i in range(devices)])  12.6 us
    all_to_all x1, starting transfers between devices, on_device(): lax.all_to_all(sent_grad, 'expert', split_axis=0, concat_axis=0, tiled=True)  12.2 us
  transfers between devices with their start and end apart: 6, of which 6 were waited for; matrix products, arithmetic and copies ran while one was open for 11% of the time, Pallas kernels for 0%

commit v1 on v0

v1 whole, which is shorter than its diff:
```python
import functools

import jax
import jax.numpy as jnp
from jax import lax
from jax.experimental import pallas as pl
from jax.experimental.pallas import tpu as pltpu
from jax.sharding import PartitionSpec as P

MESH = pl.DeviceIdType.MESH
EXPERTS = 8
GROUP = 4
MAIN = 16
REST = 4
BF = jnp.bfloat16
F32 = jnp.float32


def dot(a, b, ca=1, cb=0):
    return lax.dot_general(a, b, (((ca,), (cb,)), ((), ())), preferred_element_type=F32)


def places(routes, gates, shift):
    tokens = routes.shape[0]
    rows_main, rows_mix = EXPERTS * MAIN, EXPERTS * 2 * REST
    lanes = lax.broadcasted_iota(jnp.int32, (tokens, 128), 1)
    names = [routes[:, k : k + 1] for k in range(2)]
    onehot = [(name == lanes).astype(F32) for name in names]
    row = lax.broadcasted_iota(jnp.int32, (tokens, tokens), 0)
    column = lax.broadcasted_iota(jnp.int32, (tokens, tokens), 1)
    before = dot((column < row).astype(BF), (onehot[0] + onehot[1]).astype(BF))
    main_at = lax.broadcasted_iota(jnp.int32, (tokens, rows_main), 1)
    mix_at = lax.broadcasted_iota(jnp.int32, (tokens, rows_mix), 1)
    sel = [jnp.zeros((tokens, rows_main), F32), jnp.zeros((tokens, rows_mix), F32)]
    comb = list(sel)
    for k in range(2):
        slot = jnp.sum(onehot[k] * before, axis=1, keepdims=True).astype(jnp.int32)
        gate = gates[:, k : k + 1].astype(F32) * (1.0 / 128.0)
        in_main = jnp.where(slot < MAIN, names[k] * MAIN + slot, -1)
        in_mix = jnp.where(slot < MAIN, -1, names[k] * (2 * REST) + shift + slot - MAIN)
        for i, hit in enumerate(((main_at == in_main), (mix_at == in_mix))):
            hit = hit.astype(F32)
            sel[i] = sel[i] + hit
            comb[i] = comb[i] + hit * gate
    return [s.T.astype(BF) for s in sel] + [c.astype(BF) for c in comb]


def kernel(
    n_pipe, n_expert,
    acts, grads, routes_f, gate_f, routes_b, gate_b, saved, gate_up, down,
    moe_out, input_grad,
    x_in, g_in, w_gu, w_d, sv,
    s_f, s_b, s_m, r_f, r_b, r_m,
    x_f, x_b, acc_f, acc_b,
    pipe_s, pipe_r, loc, plane_s, plane_r, z_s, z_r, z_l, q_s, q_r, q_l,
):
    width = acts.shape[1]
    hid = down.shape[0]
    pipe = lax.axis_index("pipe")
    me = lax.axis_index("expert")
    z = me // GROUP
    line = lax.rem(me, GROUP)
    nxt = {"pipe": lax.rem(pipe + 1, n_pipe)}
    prv = {"pipe": lax.rem(pipe + n_pipe - 1, n_pipe)}
    core = 1 - 2 * lax.rem(me, 2)
    side = 2 - 4 * lax.rem(me // 2, 2)
    mates = {1: me + core, 2: me + side, 3: me + core + side}

    def along(d):
        return lax.rem(z + d, EXPERTS)

    order = (4, 3, 5, 2, 6, 1, 7)
    partners = [nxt, prv] + [{"expert": mates[r]} for r in (1, 2, 3)]
    partners += [{"expert": along(d) * GROUP + line} for d in order]
    barrier = pltpu.get_barrier_semaphore()
    for partner in partners:
        pl.semaphore_signal(barrier, inc=1, device_id=partner, device_id_type=MESH)
    pl.semaphore_wait(barrier, len(partners))

    def remote(src, dst, ssem, rsem, to):
        return pltpu.make_async_remote_copy(
            src_ref=src, dst_ref=dst, send_sem=ssem, recv_sem=rsem, device_id=to, device_id_type=MESH
        )

    shift_f = remote(acts, x_in, pipe_s.at[0], pipe_r.at[0], nxt)
    shift_b = remote(grads, g_in, pipe_s.at[1], pipe_r.at[1], prv)
    shift_f.start()
    shift_b.start()

    half = gate_up.shape[0] // 2
    parts = [pl.ds(0, half), pl.ds(half, half)]

    def send_down(src, r, by):
        return remote(src, w_d.at[r], plane_s.at[r, 0], plane_r.at[r, 0], {"expert": mates[by]})

    def send_gu(src, r, by, i):
        return remote(src.at[parts[i]], w_gu.at[r, parts[i]], plane_s.at[r, 1 + i], plane_r.at[r, 1 + i], {"expert": mates[by]})

    def saved_to(r):
        to = mates[r]
        return remote(saved.at[lax.rem(to, GROUP)], sv.at[r], plane_s.at[r, 3], plane_r.at[r, 3], {"expert": to})

    own = [
        pltpu.make_async_copy(down, w_d.at[0], loc.at[0]),
        pltpu.make_async_copy(gate_up, w_gu.at[0], loc.at[1]),
        pltpu.make_async_copy(saved.at[line], sv.at[0], loc.at[2]),
    ]
    for copy in own:
        copy.start()
    across = {(2, 0): send_down(down, 2, 2), (2, 1): send_gu(gate_up, 2, 2, 0), (2, 2): send_gu(gate_up, 2, 2, 1)}
    beside = {(1, 0): send_down(down, 1, 1), (1, 1): send_gu(gate_up, 1, 1, 0), (1, 2): send_gu(gate_up, 1, 1, 1)}
    relayed = {(3, 0): send_down(w_d.at[2], 3, 1), (3, 1): send_gu(w_gu.at[2], 3, 1, 0), (3, 2): send_gu(w_gu.at[2], 3, 1, 1)}
    kept = {r: saved_to(r) for r in (1, 2, 3)}
    for copy in across.values():
        copy.start()
    for copy in beside.values():
        copy.start()
    for copy in kept.values():
        copy.start()

    sel_f, mix_f, comb_f, cmix_f = places(routes_f[...], gate_f[...], 0)
    sel_b, mix_b, comb_b, cmix_b = places(routes_b[...], gate_b[...], REST)

    step = 512
    chunks = width // step

    def columns(i):
        return pl.ds(pl.multiple_of(i * step, step), step)

    def travel(src, dst, sems, b, d):
        ssem, rsem = sems
        there = along(d)
        return remote(src.at[there], dst.at[z], ssem.at[b, d], rsem.at[b, d], {"expert": there * GROUP + line})

    def arrive(src, dst, sems, b, d):
        ssem, rsem = sems
        there = along(EXPERTS - d)
        return remote(src.at[there], dst.at[there], ssem.at[b, d], rsem.at[b, d], {"expert": there * GROUP + line})

    out_sems, back_sems = (z_s, z_r), (q_s, q_r)

    def start_all(src, dst, sems, local_sem, b):
        for d in order:
            travel(src, dst, sems, b, d).start()
        pltpu.make_async_copy(src.at[z], dst.at[z], local_sem.at[b]).start()

    def recv_all(src, dst, sems, local_sem, b):
        for d in order[::-1]:
            arrive(src, dst, sems, b, d).wait_recv()
        pltpu.make_async_copy(src.at[z], dst.at[z], local_sem.at[b]).wait()

    def sent_all(src, dst, sems, b):
        for d in order:
            travel(src, dst, sems, b, d).wait_send()

    shift_f.wait_recv()

    @pl.loop(0, chunks)
    def _(i):
        at = columns(i)
        s_f[:, :, at] = dot(sel_f, x_in[:, at]).astype(BF).reshape(EXPERTS, MAIN, step)

    start_all(s_f, r_f, out_sems, z_l, 0)
    shift_b.wait_recv()

    @pl.loop(0, chunks)
    def _(i):
        at = columns(i)
        s_b[:, :, at] = dot(sel_b, g_in[:, at]).astype(BF).reshape(EXPERTS, MAIN, step)
        both = dot(mix_f, x_in[:, at]) + dot(mix_b, g_in[:, at])
        s_m[:, :, at] = both.reshape(EXPERTS, 2 * REST, step).astype(BF)

    start_all(s_m, r_m, out_sems, z_l, 2)
    start_all(s_b, r_b, out_sems, z_l, 1)

    def relay(i):
        across[2, i].wait_recv()
        relayed[3, i].start()

    relay(0)
    for copy in own:
        copy.wait()
    for i in range(3):
        beside[1, i].wait_recv()

    def forward(r, first):
        proj = dot(x_f[...], w_gu[r])
        a, b = proj[:, :hid], proj[:, hid:]
        hidden = (a * (1.0 / (1.0 + jnp.exp(-a))) * b).astype(BF)

        @pl.loop(0, chunks)
        def _(i):
            at = columns(i)
            part = dot(hidden, w_d[r, :, at])
            acc_f[:, at] = part if first else acc_f[:, at] + part

    def backward(r, first):
        back_hidden = dot(x_b[...], w_d[r], 1, 1)
        pre = sv[r].astype(F32)
        g, u = pre[:, :hid], pre[:, hid:]
        sigma = 1.0 / (1.0 + jnp.exp(-g))
        back_pre = jnp.concatenate(
            [back_hidden * u * sigma * (1.0 + g * (1.0 - sigma)), back_hidden * g * sigma], axis=1
        ).astype(BF)

        @pl.loop(0, chunks)
        def _(i):
            at = columns(i)
            part = dot(back_pre, w_gu[r, at, :], 1, 1)
            acc_b[:, at] = part if first else acc_b[:, at] + part

    rows_main, rows_mix = EXPERTS * MAIN, EXPERTS * 2 * REST
    recv_all(s_f, r_f, out_sems, z_l, 0)
    recv_all(s_m, r_m, out_sems, z_l, 2)
    x_f[:rows_main, :] = r_f[...].reshape(rows_main, width)
    mixed = r_m[...].reshape(rows_mix, width)
    x_f[rows_main:, :] = mixed
    x_b[rows_main:, :] = mixed
    forward(0, True)
    forward(1, False)
    recv_all(s_b, r_b, out_sems, z_l, 1)
    x_b[:rows_main, :] = r_b[...].reshape(rows_main, width)
    kept[1].wait_recv()
    backward(0, True)
    backward(1, False)
    relay(1)
    relay(2)
    kept[2].wait_recv()
    forward(2, False)
    backward(2, False)
    for i in range(3):
        relayed[3, i].wait_recv()
    kept[3].wait_recv()
    for src, dst, b in ((s_f, r_f, 0), (s_m, r_m, 2), (s_b, r_b, 1)):
        sent_all(src, dst, out_sems, b)
    for d in order:
        pl.semaphore_signal(q_l.at[0], inc=1, device_id={"expert": along(d) * GROUP + line}, device_id_type=MESH)
    forward(3, False)

    @pl.loop(0, chunks)
    def _(i):
        at = columns(i)
        r_f[:, :, at] = acc_f[:rows_main, at].astype(BF).reshape(EXPERTS, MAIN, step)

    pl.semaphore_wait(q_l.at[0], len(order))
    start_all(r_f, s_f, back_sems, z_l, 0)
    backward(3, False)

    @pl.loop(0, chunks)
    def _(i):
        at = columns(i)
        r_b[:, :, at] = acc_b[:rows_main, at].astype(BF).reshape(EXPERTS, MAIN, step)
        row = lax.broadcasted_iota(jnp.int32, (rows_mix, step), 0)
        both = jnp.where(lax.rem(row, 2 * REST) < REST, acc_f[rows_main:, at], acc_b[rows_main:, at])
        r_m[:, :, at] = both.reshape(EXPERTS, 2 * REST, step).astype(BF)

    start_all(r_m, s_m, back_sems, z_l, 2)
    start_all(r_b, s_b, back_sems, z_l, 1)
    recv_all(r_f, s_f, back_sems, z_l, 0)
    recv_all(r_m, s_m, back_sems, z_l, 2)

    @pl.loop(0, chunks)
    def _(i):
        at = columns(i)
        main = s_f[:, :, at].reshape(rows_main, step)
        mix = s_m[:, :, at].reshape(rows_mix, step)
        moe_out[:, at] = (x_in[:, at].astype(F32) + dot(comb_f, main) + dot(cmix_f, mix)).astype(BF)

    recv_all(r_b, s_b, back_sems, z_l, 1)

    @pl.loop(0, chunks)
    def _(i):
        at = columns(i)
        main = s_b[:, :, at].reshape(rows_main, step)
        mix = s_m[:, :, at].reshape(rows_mix, step)
        input_grad[:, at] = (g_in[:, at].astype(F32) + dot(comb_b, main) + dot(cmix_b, mix)).astype(BF)

    for src, dst, b in ((r_f, s_f, 0), (r_m, s_m, 2), (r_b, s_b, 1)):
        sent_all(src, dst, back_sems, b)
    shift_f.wait_send()
    shift_b.wait_send()
    for copies in (across, beside, relayed, kept):
        for copy in copies.values():
            copy.wait_send()


def on_device(n_pipe, n_expert, acts, grads, routes_f, gate_f, routes_b, gate_b, saved, gate_up, down):
    tokens, width = acts.shape[1:]
    hid = down.shape[2]
    wide = gate_up.shape[3]
    rows_main, rows_mix = EXPERTS * MAIN, EXPERTS * 2 * REST
    rows = rows_main + rows_mix
    by_line = saved[0, 0].reshape(EXPERTS, GROUP, MAIN + REST, wide).transpose(1, 0, 2, 3)
    main = by_line[:, :, :MAIN].reshape(GROUP, rows_main, wide)
    mix = jnp.pad(by_line[:, :, MAIN:], ((0, 0), (0, 0), (REST, 0), (0, 0))).reshape(GROUP, rows_mix, wide)
    by_line = jnp.concatenate([main, mix], axis=1)

    vmem = pl.BlockSpec(memory_space=pltpu.VMEM)
    hbm = pl.BlockSpec(memory_space=pl.ANY)
    block = pltpu.VMEM((EXPERTS, MAIN, width), BF)
    mixed = pltpu.VMEM((EXPERTS, 2 * REST, width), BF)
    sems = pltpu.SemaphoreType.DMA
    out = jax.ShapeDtypeStruct((tokens, width), BF)
    moe_out, input_grad = pl.pallas_call(
        functools.partial(kernel, n_pipe, n_expert),
        out_shape=(out, out),
        in_specs=[hbm, hbm, vmem, vmem, vmem, vmem, hbm, hbm, hbm],
        out_specs=(vmem, vmem),
        scratch_shapes=[
            pltpu.VMEM((tokens, width), BF),
            pltpu.VMEM((tokens, width), BF),
            pltpu.VMEM((GROUP, width, wide), BF),
            pltpu.VMEM((GROUP, hid, width), BF),
            pltpu.VMEM((GROUP, rows, wide), BF),
            block, block, mixed, block, block, mixed,
            pltpu.VMEM((rows, width), BF),
            pltpu.VMEM((rows, width), BF),
            pltpu.VMEM((rows, width), F32),
            pltpu.VMEM((rows, width), F32),
            sems((2,)), sems((2,)), sems((3,)),
            sems((GROUP, 4)), sems((GROUP, 4)),
            sems((3, EXPERTS)), sems((3, EXPERTS)), sems((3,)),
            sems((3, EXPERTS)), sems((3, EXPERTS)),
            pltpu.SemaphoreType.REGULAR((1,)),
        ],
        compiler_params=pltpu.CompilerParams(
            collective_id=0, has_side_effects=True, vmem_limit_bytes=60 * 1024 * 1024
        ),
    )(acts[0], grads[0], routes_f[0], gate_f[0], routes_b[0], gate_b[0], by_line, gate_up[0, 0], down[0, 0])
    return moe_out[None], input_grad[None]


def solution(mesh):
    three = P("pipe", "expert", None)
    four = P("pipe", "expert", None, None)
    return jax.shard_map(
        functools.partial(on_device, mesh.shape["pipe"], mesh.shape["expert"]),
        mesh=mesh,
        in_specs=(three,) * 6 + (P("pipe", "expert", None, None, None), four, four),
        out_specs=(three, three),
        check_vma=False,
    )
```

time: 431 us -> 154 us (0.36)
  waiting for transfers between devices: 319 us -> 0 us
  Pallas kernels: 0 us -> 141 us
  starting transfers between devices: 39.7 us -> 0 us
  local copies, waits for them, and re-layouts: 40.2 us -> 10.4 us
  matrix products: 16.3 us -> 0 us
  other arithmetic: 14.3 us -> 0.88 us
    all_to_all x4 -> x0, waiting for transfers between devices: 292 us -> none  [the longest x1 85.9 us: on_device(): lax.all_to_all(fwd_part.reshape(blocks, capacity, model_width), 'expert',...]
    pallas_call x0 -> x1, Pallas kernels: none -> 141 us  [on_device(): pl.pallas_call(functools.partial(kernel, n_pipe, n_expert), out_shape=(ou...]
    all_to_all x4 -> x0, starting transfers between devices: 27 us -> none  [the longest x1 12.2 us: on_device(): lax.all_to_all(sent_grad, 'expert', split_axis=0, concat_axis=0, tiled=True)]
    ppermute x2 -> x0, waiting for transfers between devices: 27 us -> none  [from_behind(): lax.ppermute(array, axis, [(i, (i + by) % devices) for i in range(devices)])]
    reshape x10 -> x1, local copies, waits for them, and re-layouts: 25.6 us -> 0.06 us  [on_device(): jnp.pad(by_line[:, :, MAIN:], ((0, 0), (0, 0), (REST, 0), (0, 0)))]
    dot_general x6 -> x0, matrix products: 16.3 us -> none  [the longest x1 3.73 us: expert_work(): projected = jnp.dot(rows_in, inner_w, preferred_element_type=jnp.float32)]
    ppermute x2 -> x0, starting transfers between devices: 12.6 us -> none  [from_behind(): lax.ppermute(array, axis, [(i, (i + by) % devices) for i in range(devices)])]
    reduce_sum x6 -> x0, other arithmetic: 10.8 us -> none  [the longest x2 4.97 us: combine_rows(): jnp.sum(picked * weights[..., None], axis=1)]
  transfers between devices with their start and end apart: 6 -> 0, of which waited for: 6 -> 0; matrix products, arithmetic and copies ran while one was open for 11% -> 0% of each run, Pallas kernels for 0% -> 0%
where the time goes in v1:
time: 154 us; the launch traced here: 153 us
  Pallas kernels  141 us (92%)
  local copies, waits for them, and re-layouts  10.4 us (7%)
    pallas_call x1, Pallas kernels, on_device(): pl.pallas_call(functools.partial(kernel, n_pipe, n_expert), out_shape=(ou...  141 us
    unnamed x2, local copies, waits for them, and re-layouts  3.44 us

profile of v1, /device:TPU:1, one launch (start us, length us, event | category | flops | bytes accessed | tf_op | source)
XLA Modules:
  0.0 153.3 jit_solution(5915607754295035476)
XLA Ops:
  0.6 1.4 copy.12.routes_f
  2.0 1.4 copy.13.gate_f
  3.4 1.4 copy.14.routes_b
  4.8 1.4 copy.15.gate_b
  6.1 1.1 reshape_squeeze.3
  7.3 0.2 copy.17
  7.6 0.1 pad_bitcast_fusion
  7.6 0.9 pad_maximum_fusion.saved
  8.5 141.3 %shard_map.104 = (bf16[64,2560]{1,0:T(8,128)(2,1)}, bf16[64,2560]{1,0:T(8,128)(2,1)}) custom-call(bf16[64,2560]{1,0:T(8,128)(2,1)} %bitcast.25, bf16[64,2560]{1,0:T(8,128)(2,1)} %bitcast.26, s32[64,2]{1,0:T(8,128)} %copy.12.routes_f, s32[64,2]{1,0:T(8,128)} %copy.13.gate_f, s32[64,2]{1,0:T(8,128)} %copy.14.routes_b, s32[64,2]{1,0:T(8,128)} %copy.15.gate_b, ...), custom_call_target="tpu_custom_call" | custom-call | tf_op jit(solution)/shard_map/pallas_call | solution.py:304
  149.8 1.7 %copy.20 = bf16[1,64,2560]{2,1,0:T(8,128)(2,1)} copy(bf16[1,64,2560]{2,1,0:T(8,128)(2,1)} %bitcast.28) | data formatting | bytes 655360
  151.6 1.7 %copy.21 = bf16[1,64,2560]{2,1,0:T(8,128)(2,1)} copy(bf16[1,64,2560]{2,1,0:T(8,128)(2,1)} %bitcast.27) | data formatting | bytes 655360
  (2 shorter events, 0.1 us)

commit v2 on v1

v2 whole, which is shorter than its diff:
```python
import functools

import jax
import jax.numpy as jnp
from jax import lax
from jax.experimental import pallas as pl
from jax.experimental.pallas import tpu as pltpu
from jax.sharding import PartitionSpec as P

MESH = pl.DeviceIdType.MESH
EXPERTS = 8
GROUP = 4
MAIN = 16
REST = 4
BF = jnp.bfloat16
F32 = jnp.float32
ROWS_MAIN = EXPERTS * MAIN
ROWS_MIX = EXPERTS * 2 * REST
ROWS = ROWS_MAIN + ROWS_MIX
CHUNKS = 4


def dot(a, b, ca=1, cb=0):
    return lax.dot_general(a, b, (((ca,), (cb,)), ((), ())), preferred_element_type=F32)


def places(routes, gates, shift):
    tokens = routes.shape[1]
    names = [routes[k : k + 1, :] for k in range(2)]
    experts = lax.broadcasted_iota(jnp.int32, (EXPERTS, tokens), 0)
    onehot = [(name == experts).astype(F32) for name in names]
    row = lax.broadcasted_iota(jnp.int32, (tokens, tokens), 0)
    column = lax.broadcasted_iota(jnp.int32, (tokens, tokens), 1)
    before = dot((onehot[0] + onehot[1]).astype(BF), (row < column).astype(BF))
    sel = [jnp.zeros((rows, tokens), F32) for rows in (ROWS_MAIN, ROWS_MIX)]
    at = [lax.broadcasted_iota(jnp.int32, s.shape, 0) for s in sel]
    comb = list(sel)
    for k in range(2):
        slot = jnp.sum(onehot[k] * before, axis=0, keepdims=True).astype(jnp.int32)
        gate = gates[k : k + 1, :].astype(F32) * (1.0 / 128.0)
        in_main = jnp.where(slot < MAIN, names[k] * MAIN + slot, -1)
        in_mix = jnp.where(slot < MAIN, -1, names[k] * (2 * REST) + shift + slot - MAIN)
        for i, place in enumerate((in_main, in_mix)):
            hit = (at[i] == place).astype(F32)
            sel[i] = sel[i] + hit
            comb[i] = comb[i] + hit * gate
    return [s.astype(BF) for s in sel] + [c.T.astype(BF) for c in comb]


def kernel(
    n_pipe,
    acts, grads, routes_f, gate_f, routes_b, gate_b, saved, gate_up, down,
    moe_out, input_grad,
    x_in, g_in, w_gu, w_d, raw, sv_out, sv,
    s_f, s_b, s_m, r_f, r_b, r_m,
    y_f, y_b, y_m, h_f, h_b, h_m,
    x_f, x_b, pre_b, proj_f, hid_f,
    pipe_s, pipe_r, loc, plane_s, plane_r, z_s, z_r, z_l, q_s, q_r, q_l,
):
    width = acts.shape[1]
    hid = down.shape[0]
    step = width // CHUNKS
    pipe = lax.axis_index("pipe")
    me = lax.axis_index("expert")
    z = me // GROUP
    line = lax.rem(me, GROUP)
    nxt = {"pipe": lax.rem(pipe + 1, n_pipe)}
    prv = {"pipe": lax.rem(pipe + n_pipe - 1, n_pipe)}
    core = 1 - 2 * lax.rem(me, 2)
    side = 2 - 4 * lax.rem(me // 2, 2)
    mates = {1: me + core, 2: me + side, 3: me + core + side}

    def along(d):
        return lax.rem(z + d, EXPERTS)

    order = (4, 3, 5, 2, 6, 1, 7)
    load_raw = pltpu.make_async_copy(saved, raw, loc.at[3])
    load_raw.start()
    own = [
        pltpu.make_async_copy(down, w_d.at[0], loc.at[0]),
        pltpu.make_async_copy(gate_up, w_gu.at[0], loc.at[1]),
    ]
    for copy in own:
        copy.start()
    partners = [nxt, prv] + [{"expert": mates[r]} for r in (1, 2, 3)]
    partners += [{"expert": along(d) * GROUP + line} for d in order]
    barrier = pltpu.get_barrier_semaphore()
    for partner in partners:
        pl.semaphore_signal(barrier, inc=1, device_id=partner, device_id_type=MESH)
    pl.semaphore_wait(barrier, len(partners))

    def remote(src, dst, ssem, rsem, to):
        return pltpu.make_async_remote_copy(
            src_ref=src, dst_ref=dst, send_sem=ssem, recv_sem=rsem, device_id=to, device_id_type=MESH
        )

    shift_f = remote(acts, x_in, pipe_s.at[0], pipe_r.at[0], nxt)
    shift_b = remote(grads, g_in, pipe_s.at[1], pipe_r.at[1], prv)
    shift_b.start()
    shift_f.start()

    parts = [pl.ds(i * step, step) for i in range(CHUNKS)]

    def send_down(src, r, by):
        return remote(src, w_d.at[r], plane_s.at[r, 0], plane_r.at[r, 0], {"expert": mates[by]})

    def send_gu(src, r, by, i):
        at = 2 + i
        return remote(src.at[parts[i]], w_gu.at[r, parts[i]], plane_s.at[r, at], plane_r.at[r, at], {"expert": mates[by]})

    def saved_to(r):
        to = mates[r]
        return remote(sv_out.at[lax.rem(to, GROUP)], sv.at[r], plane_s.at[r, 1], plane_r.at[r, 1], {"expert": to})

    downs = {1: send_down(down, 1, 1), 2: send_down(down, 2, 2), 3: send_down(w_d.at[2], 3, 1)}
    gus = {1: [send_gu(gate_up, 1, 1, i) for i in range(CHUNKS)]}
    gus[2] = [send_gu(gate_up, 2, 2, i) for i in range(CHUNKS)]
    gus[3] = [send_gu(w_gu.at[2], 3, 1, i) for i in range(CHUNKS)]
    kept = {r: saved_to(r) for r in (1, 2, 3)}
    downs[2].start()
    downs[1].start()

    load_raw.wait()
    flat = raw[...].reshape(raw.shape[0] * raw.shape[1], raw.shape[2])
    row = lax.broadcasted_iota(jnp.int32, (ROWS, flat.shape[0]), 0)
    column = lax.broadcasted_iota(jnp.int32, (ROWS, flat.shape[0]), 1)
    late = row - ROWS_MAIN
    slot = jnp.where(late < 0, row & (MAIN - 1), MAIN - REST + (late & (2 * REST - 1)))
    plane = jnp.where(late < 0, row >> 4, late >> 3)
    known = (late < 0) | (slot >= MAIN)
    base = jnp.where(known, slot * raw.shape[1] + plane * GROUP, -GROUP)
    for number in range(GROUP):
        pick = (column == base + number).astype(BF)
        sv_out[number] = dot(pick, flat).astype(BF)
    keep_own = pltpu.make_async_copy(sv_out.at[line], sv.at[0], loc.at[2])
    keep_own.start()
    for r in (2, 3, 1):
        kept[r].start()
    for i in range(CHUNKS):
        gus[2][i].start()
        gus[1][i].start()

    sel_f, mix_f, comb_f, cmix_f = places(routes_f[...], gate_f[...], 0)
    sel_b, mix_b, comb_b, cmix_b = places(routes_b[...], gate_b[...], REST)

    def columns(i):
        return pl.ds(pl.multiple_of(i * step, step), step)

    everything = pl.ds(0, width)

    def travel(src, dst, sems, b, d, at):
        ssem, rsem = sems
        there = along(d)
        return remote(
            src.at[there, :, at], dst.at[z, :, at], ssem.at[b, d], rsem.at[b, d], {"expert": there * GROUP + line}
        )

    def arrive(src, dst, sems, b, d, at):
        ssem, rsem = sems
        there = along(EXPERTS - d)
        return remote(
            src.at[there, :, at], dst.at[there, :, at], ssem.at[b, d], rsem.at[b, d], {"expert": there * GROUP + line}
        )

    def start_all(src, dst, sems, local_sem, b, at):
        for d in order:
            travel(src, dst, sems, b, d, at).start()
        pltpu.make_async_copy(src.at[z, :, at], dst.at[z, :, at], local_sem.at[b]).start()

    def recv_all(src, dst, sems, local_sem, b, at):
        for d in order[::-1]:
            arrive(src, dst, sems, b, d, at).wait_recv()
        pltpu.make_async_copy(src.at[z, :, at], dst.at[z, :, at], local_sem.at[b]).wait()

    def sent_all(src, dst, sems, b, at):
        for d in order:
            travel(src, dst, sems, b, d, at).wait_send()

    out_sems, back_sems = (z_s, z_r), (q_s, q_r)

    shift_b.wait_recv()

    @pl.loop(0, CHUNKS)
    def _(i):
        at = columns(i)
        s_b[:, :, at] = dot(sel_b, g_in[:, at]).astype(BF).reshape(EXPERTS, MAIN, step)

    start_all(s_b, r_b, out_sems, z_l, 1, everything)
    shift_f.wait_recv()

    @pl.loop(0, CHUNKS)
    def _(i):
        at = columns(i)
        both = dot(mix_f, x_in[:, at]) + dot(mix_b, g_in[:, at])
        s_m[:, :, at] = both.reshape(EXPERTS, 2 * REST, step).astype(BF)

    start_all(s_m, r_m, out_sems, z_l, 2, everything)

    @pl.loop(0, CHUNKS)
    def _(i):
        at = columns(i)
        s_f[:, :, at] = dot(sel_f, x_in[:, at]).astype(BF).reshape(EXPERTS, MAIN, step)

    start_all(s_f, r_f, out_sems, z_l, 0, everything)

    for copy in own:
        copy.wait()
    keep_own.wait()
    downs[2].wait_recv()
    downs[3].start()
    recv_all(s_b, r_b, out_sems, z_l, 1, everything)
    x_b[:ROWS_MAIN, :] = r_b[...].reshape(ROWS_MAIN, width)
    recv_all(s_m, r_m, out_sems, z_l, 2, everything)
    mixed = r_m[...].reshape(ROWS_MIX, width)
    x_f[ROWS_MAIN:, :] = mixed
    x_b[ROWS_MAIN:, :] = mixed
    for r in range(GROUP):
        if r in (1, 3):
            downs[r].wait_recv()
        if r:
            kept[r].wait_recv()
        back_hidden = dot(x_b[...], w_d[r], 1, 1)
        pre = sv[r].astype(F32)
        g, u = pre[:, :hid], pre[:, hid:]
        sigma = 1.0 / (1.0 + jnp.exp(-g))
        pre_b[r] = jnp.concatenate(
            [back_hidden * u * sigma * (1.0 + g * (1.0 - sigma)), back_hidden * g * sigma], axis=1
        ).astype(BF)

    def backward(i):
        at = parts[i]
        gus[2][i].wait_recv()
        gus[3][i].start()
        gus[1][i].wait_recv()
        total = dot(pre_b[0], w_gu[0, at, :], 1, 1)
        total = total + dot(pre_b[1], w_gu[1, at, :], 1, 1)
        total = total + dot(pre_b[2], w_gu[2, at, :], 1, 1)
        gus[3][i].wait_recv()
        total = total + dot(pre_b[3], w_gu[3, at, :], 1, 1)
        y_b[:, :, at] = total[:ROWS_MAIN].astype(BF).reshape(EXPERTS, MAIN, step)
        y_m[:, :, at] = total[ROWS_MAIN:].astype(BF).reshape(EXPERTS, 2 * REST, step)
        start_all(y_b, h_b, back_sems, q_l, 2 * CHUNKS + i, at)

    def project(i):
        at = parts[i]
        for r in range(GROUP):
            part = dot(x_f[:, at], w_gu[r, at, :])
            proj_f[r] = part if i == 0 else proj_f[r] + part

    for i in range(CHUNKS):
        backward(i)
        if i == 1:
            recv_all(s_f, r_f, out_sems, z_l, 0, everything)
            x_f[:ROWS_MAIN, :] = r_f[...].reshape(ROWS_MAIN, width)
            project(0)
        if i:
            project(i)
    for r in range(GROUP):
        a, b = proj_f[r, :, :hid], proj_f[r, :, hid:]
        hid_f[r] = (a * (1.0 / (1.0 + jnp.exp(-a))) * b).astype(BF)
    from_forward = (lax.broadcasted_iota(jnp.int32, (ROWS_MIX, step), 0) & (2 * REST - 1)) < REST
    for i in range(CHUNKS):
        at = parts[i]
        total = dot(hid_f[0], w_d[0, :, at])
        for r in range(1, GROUP):
            total = total + dot(hid_f[r], w_d[r, :, at])
        y_f[:, :, at] = total[:ROWS_MAIN].astype(BF).reshape(EXPERTS, MAIN, step)
        other = y_m[:, :, at].reshape(ROWS_MIX, step).astype(F32)
        y_m[:, :, at] = (
            jnp.where(from_forward, total[ROWS_MAIN:], other).reshape(EXPERTS, 2 * REST, step).astype(BF)
        )
        start_all(y_f, h_f, back_sems, q_l, i, at)
        start_all(y_m, h_m, back_sems, q_l, CHUNKS + i, at)

    for i in range(CHUNKS):
        recv_all(y_b, h_b, back_sems, q_l, 2 * CHUNKS + i, parts[i])
    for i in range(CHUNKS):
        at = parts[i]
        recv_all(y_f, h_f, back_sems, q_l, i, at)
        recv_all(y_m, h_m, back_sems, q_l, CHUNKS + i, at)
        mix = h_m[:, :, at].reshape(ROWS_MIX, step)
        main = h_f[:, :, at].reshape(ROWS_MAIN, step)
        moe_out[:, at] = (x_in[:, at].astype(F32) + dot(comb_f, main) + dot(cmix_f, mix)).astype(BF)
        main = h_b[:, :, at].reshape(ROWS_MAIN, step)
        input_grad[:, at] = (g_in[:, at].astype(F32) + dot(comb_b, main) + dot(cmix_b, mix)).astype(BF)

    for src, dst, b in ((s_f, r_f, 0), (s_b, r_b, 1), (s_m, r_m, 2)):
        sent_all(src, dst, out_sems, b, everything)
    for i in range(CHUNKS):
        for src, dst, b in ((y_f, h_f, 0), (y_m, h_m, 1), (y_b, h_b, 2)):
            sent_all(src, dst, back_sems, b * CHUNKS + i, parts[i])
    shift_f.wait_send()
    shift_b.wait_send()
    for r in (1, 2, 3):
        downs[r].wait_send()
        kept[r].wait_send()
        for copy in gus[r]:
            copy.wait_send()


def write_out(a, b, out_a, out_b, sem):
    copies = [pltpu.make_async_copy(a, out_a, sem.at[0]), pltpu.make_async_copy(b, out_b, sem.at[1])]
    for copy in copies:
        copy.start()
    for copy in copies:
        copy.wait()


def on_device(n_pipe, acts, grads, routes_f, gate_f, routes_b, gate_b, saved, gate_up, down):
    tokens, width = acts.shape[1:]
    hid = down.shape[2]
    wide = gate_up.shape[3]
    vmem = pl.BlockSpec(memory_space=pltpu.VMEM)
    hbm = pl.BlockSpec(memory_space=pl.ANY)
    block = pltpu.VMEM((EXPERTS, MAIN, width), BF)
    mixed = pltpu.VMEM((EXPERTS, 2 * REST, width), BF)
    sems = pltpu.SemaphoreType.DMA
    out = jax.ShapeDtypeStruct((tokens, width), BF)
    by_slot = saved[0, 0].transpose(1, 0, 2)
    results = pl.pallas_call(
        functools.partial(kernel, n_pipe),
        out_shape=(out, out),
        in_specs=[hbm, hbm, vmem, vmem, vmem, vmem, hbm, hbm, hbm],
        out_specs=(vmem, vmem),
        scratch_shapes=[
            pltpu.VMEM((tokens, width), BF),
            pltpu.VMEM((tokens, width), BF),
            pltpu.VMEM((GROUP, width, wide), BF),
            pltpu.VMEM((GROUP, hid, width), BF),
            pltpu.VMEM(by_slot.shape, BF),
            pltpu.VMEM((GROUP, ROWS, wide), BF),
            pltpu.VMEM((GROUP, ROWS, wide), BF),
            block, block, mixed, block, block, mixed,
            block, block, mixed, block, block, mixed,
            pltpu.VMEM((ROWS, width), BF),
            pltpu.VMEM((ROWS, width), BF),
            pltpu.VMEM((GROUP, ROWS, wide), BF),
            pltpu.VMEM((GROUP, ROWS, wide), F32),
            pltpu.VMEM((GROUP, ROWS, hid), BF),
            sems((2,)), sems((2,)), sems((4,)),
            sems((GROUP, 2 + CHUNKS)), sems((GROUP, 2 + CHUNKS)),
            sems((3, EXPERTS)), sems((3, EXPERTS)), sems((3,)),
            sems((3 * CHUNKS, EXPERTS)), sems((3 * CHUNKS, EXPERTS)), sems((3 * CHUNKS,)),
        ],
        compiler_params=pltpu.CompilerParams(
            collective_id=0, has_side_effects=True, vmem_limit_bytes=60 * 1024 * 1024
        ),
    )(
        acts[0], grads[0], routes_f[0].T, gate_f[0].T, routes_b[0].T, gate_b[0].T,
        by_slot, gate_up[0, 0], down[0, 0],
    )
    moe_out, input_grad = pl.pallas_call(
        write_out,
        out_shape=(out, out),
        in_specs=[vmem, vmem],
        out_specs=(hbm, hbm),
        scratch_shapes=[sems((2,))],
    )(*results)
    return moe_out[None], input_grad[None]


def solution(mesh):
    three = P("pipe", "expert", None)
    four = P("pipe", "expert", None, None)
    return jax.shard_map(
        functools.partial(on_device, mesh.shape["pipe"]),
        mesh=mesh,
        in_specs=(three,) * 6 + (P("pipe", "expert", None, None, None), four, four),
        out_specs=(three, three),
        check_vma=False,
    )
```

time: 154 us -> 135 us (0.88)
  local copies, waits for them, and re-layouts: 10.4 us -> 0 us
  Pallas kernels: 141 us -> 134 us
    pallas_call x1 -> x2, Pallas kernels: 141 us -> 134 us  [the longest x1 132 us: on_device(): pl.pallas_call(functools.partial(kernel, n_pipe), out_shape=(out, out), i...]
    squeeze x4 -> x0, local copies, waits for them, and re-layouts: 5.51 us -> none  [the longest x1 1.38 us: on_device(): routes_f[0]]
    unnamed x2 -> x0, local copies, waits for them, and re-layouts: 3.44 us -> none
where the time goes in v2:
time: 135 us
  Pallas kernels  134 us (99%)
    pallas_call x1, Pallas kernels, on_device(): pl.pallas_call(functools.partial(kernel, n_pipe), out_shape=(out, out), i...  132 us

profile of v2, /device:TPU:1, one launch (start us, length us, event | category | flops | bytes accessed | tf_op | source)
XLA Modules:
  0.0 134.6 jit_solution(10445105880186566154)
XLA Ops:
  0.6 132.1 %shard_map.104 = (bf16[64,2560]{1,0:T(8,128)(2,1)}, bf16[64,2560]{1,0:T(8,128)(2,1)}) custom-call(bf16[64,2560]{1,0:T(8,128)(2,1)} %bitcast.24, bf16[64,2560]{1,0:T(8,128)(2,1)} %bitcast.25, s32[2,64]{1,0:T(2,128)} %bitcast.26, s32[2,64]{1,0:T(2,128)} %bitcast.27, s32[2,64]{1,0:T(2,128)} %bitcast.28, s32[2,64]{1,0:T(2,128)} %bitcast.29, ...), custom_call_target="tpu_custom_call" | custom-call | tf_op jit(solution)/shard_map/pallas_call | solution.py:320
  132.7 1.9 %shard_map.105 = (bf16[64,2560]{1,0:T(8,128)(2,1)}, bf16[64,2560]{1,0:T(8,128)(2,1)}) custom-call(bf16[64,2560]{1,0:T(8,128)(2,1)} %get-tuple-element.6.a, bf16[64,2560]{1,0:T(8,128)(2,1)} %get-tuple-element.7.b), custom_call_target="tpu_custom_call" | custom-call | tf_op jit(solution)/shard_map/pallas_call | solution.py:352

commit v3 on v2

--- a/solution.py
+++ b/solution.py
@@ -17,7 +17,9 @@
 ROWS_MAIN = EXPERTS * MAIN
 ROWS_MIX = EXPERTS * 2 * REST
 ROWS = ROWS_MAIN + ROWS_MIX
-CHUNKS = 4
+PARTS = (768, 768, 640, 384)
+CHUNKS = len(PARTS)
+STEPS = 4
 
 
 def dot(a, b, ca=1, cb=0):
@@ -55,20 +57,22 @@
     s_f, s_b, s_m, r_f, r_b, r_m,
     y_f, y_b, y_m, h_f, h_b, h_m,
     x_f, x_b, pre_b, proj_f, hid_f,
-    pipe_s, pipe_r, loc, plane_s, plane_r, z_s, z_r, z_l, q_s, q_r, q_l,
+    meta, o_f, o_b, fin_f, fin_b,
+    pipe_s, pipe_r, loc, plane_s, plane_r, z_s, z_r, z_l, q_s, q_r, q_l, fin_s, fin_r, meta_s, meta_r,
 ):
     width = acts.shape[1]
     hid = down.shape[0]
-    step = width // CHUNKS
+    step = width // STEPS
     pipe = lax.axis_index("pipe")
     me = lax.axis_index("expert")
     z = me // GROUP
     line = lax.rem(me, GROUP)
-    nxt = {"pipe": lax.rem(pipe + 1, n_pipe)}
-    prv = {"pipe": lax.rem(pipe + n_pipe - 1, n_pipe)}
     core = 1 - 2 * lax.rem(me, 2)
     side = 2 - 4 * lax.rem(me // 2, 2)
-    mates = {1: me + core, 2: me + side, 3: me + core + side}
+    mates = {0: me, 1: me + core, 2: me + side, 3: me + core + side}
+    nxt = {"pipe": lax.rem(pipe + 1, n_pipe), "expert": mates[2]}
+    prv = {"pipe": lax.rem(pipe + n_pipe - 1, n_pipe), "expert": mates[2]}
+    pair = {"expert": mates[2]}
 
     def along(d):
         return lax.rem(z + d, EXPERTS)
@@ -96,10 +100,16 @@
 
     shift_f = remote(acts, x_in, pipe_s.at[0], pipe_r.at[0], nxt)
     shift_b = remote(grads, g_in, pipe_s.at[1], pipe_r.at[1], prv)
+    tables = [
+        remote(table, meta.at[k], meta_s.at[k], meta_r.at[k], pair)
+        for k, table in enumerate((routes_f, gate_f, routes_b, gate_b))
+    ]
+    for copy in tables:
+        copy.start()
     shift_b.start()
     shift_f.start()
 
-    parts = [pl.ds(i * step, step) for i in range(CHUNKS)]
+    parts = [pl.ds(sum(PARTS[:i]), PARTS[i]) for i in range(CHUNKS)]
 
     def send_down(src, r, by):
         return remote(src, w_d.at[r], plane_s.at[r, 0], plane_r.at[r, 0], {"expert": mates[by]})
@@ -110,7 +120,7 @@
 
     def saved_to(r):
         to = mates[r]
-        return remote(sv_out.at[lax.rem(to, GROUP)], sv.at[r], plane_s.at[r, 1], plane_r.at[r, 1], {"expert": to})
+        return remote(sv_out.at[lax.rem(mates[r ^ 2], GROUP)], sv.at[r], plane_s.at[r, 1], plane_r.at[r, 1], {"expert": to})
 
     downs = {1: send_down(down, 1, 1), 2: send_down(down, 2, 2), 3: send_down(w_d.at[2], 3, 1)}
     gus = {1: [send_gu(gate_up, 1, 1, i) for i in range(CHUNKS)]}
@@ -132,7 +142,7 @@
     for number in range(GROUP):
         pick = (column == base + number).astype(BF)
         sv_out[number] = dot(pick, flat).astype(BF)
-    keep_own = pltpu.make_async_copy(sv_out.at[line], sv.at[0], loc.at[2])
+    keep_own = pltpu.make_async_copy(sv_out.at[lax.rem(mates[2], GROUP)], sv.at[0], loc.at[2])
     keep_own.start()
     for r in (2, 3, 1):
         kept[r].start()
@@ -140,8 +150,10 @@
         gus[2][i].start()
         gus[1][i].start()
 
-    sel_f, mix_f, comb_f, cmix_f = places(routes_f[...], gate_f[...], 0)
-    sel_b, mix_b, comb_b, cmix_b = places(routes_b[...], gate_b[...], REST)
+    for copy in tables:
+        copy.wait_recv()
+    sel_f, mix_f, comb_f, cmix_f = places(meta[0], meta[1], 0)
+    sel_b, mix_b, comb_b, cmix_b = places(meta[2], meta[3], REST)
 
     def columns(i):
         return pl.ds(pl.multiple_of(i * step, step), step)
@@ -180,7 +192,7 @@
 
     shift_b.wait_recv()
 
-    @pl.loop(0, CHUNKS)
+    @pl.loop(0, STEPS)
     def _(i):
         at = columns(i)
         s_b[:, :, at] = dot(sel_b, g_in[:, at]).astype(BF).reshape(EXPERTS, MAIN, step)
@@ -188,7 +200,7 @@
     start_all(s_b, r_b, out_sems, z_l, 1, everything)
     shift_f.wait_recv()
 
-    @pl.loop(0, CHUNKS)
+    @pl.loop(0, STEPS)
     def _(i):
         at = columns(i)
         both = dot(mix_f, x_in[:, at]) + dot(mix_b, g_in[:, at])
@@ -196,7 +208,7 @@
 
     start_all(s_m, r_m, out_sems, z_l, 2, everything)
 
-    @pl.loop(0, CHUNKS)
+    @pl.loop(0, STEPS)
     def _(i):
         at = columns(i)
         s_f[:, :, at] = dot(sel_f, x_in[:, at]).astype(BF).reshape(EXPERTS, MAIN, step)
@@ -237,8 +249,8 @@
         total = total + dot(pre_b[2], w_gu[2, at, :], 1, 1)
         gus[3][i].wait_recv()
         total = total + dot(pre_b[3], w_gu[3, at, :], 1, 1)
-        y_b[:, :, at] = total[:ROWS_MAIN].astype(BF).reshape(EXPERTS, MAIN, step)
-        y_m[:, :, at] = total[ROWS_MAIN:].astype(BF).reshape(EXPERTS, 2 * REST, step)
+        y_b[:, :, at] = total[:ROWS_MAIN].astype(BF).reshape(EXPERTS, MAIN, PARTS[i])
+        y_m[:, :, at] = total[ROWS_MAIN:].astype(BF).reshape(EXPERTS, 2 * REST, PARTS[i])
         start_all(y_b, h_b, back_sems, q_l, 2 * CHUNKS + i, at)
 
     def project(i):
@@ -258,32 +270,52 @@
     for r in range(GROUP):
         a, b = proj_f[r, :, :hid], proj_f[r, :, hid:]
         hid_f[r] = (a * (1.0 / (1.0 + jnp.exp(-a))) * b).astype(BF)
-    from_forward = (lax.broadcasted_iota(jnp.int32, (ROWS_MIX, step), 0) & (2 * REST - 1)) < REST
-    for i in range(CHUNKS):
-        at = parts[i]
+    for i in range(CHUNKS):
+        at = parts[i]
+        shape = (ROWS_MIX, PARTS[i])
         total = dot(hid_f[0], w_d[0, :, at])
         for r in range(1, GROUP):
             total = total + dot(hid_f[r], w_d[r, :, at])
-        y_f[:, :, at] = total[:ROWS_MAIN].astype(BF).reshape(EXPERTS, MAIN, step)
-        other = y_m[:, :, at].reshape(ROWS_MIX, step).astype(F32)
-        y_m[:, :, at] = (
-            jnp.where(from_forward, total[ROWS_MAIN:], other).reshape(EXPERTS, 2 * REST, step).astype(BF)
-        )
+        y_f[:, :, at] = total[:ROWS_MAIN].astype(BF).reshape(EXPERTS, MAIN, PARTS[i])
+        from_forward = (lax.broadcasted_iota(jnp.int32, shape, 0) & (2 * REST - 1)) < REST
+        other = y_m[:, :, at].reshape(shape).astype(F32)
+        both = jnp.where(from_forward, total[ROWS_MAIN:], other)
+        y_m[:, :, at] = both.reshape(EXPERTS, 2 * REST, PARTS[i]).astype(BF)
         start_all(y_f, h_f, back_sems, q_l, i, at)
         start_all(y_m, h_m, back_sems, q_l, CHUNKS + i, at)
 
+    def finished(i):
+        at = parts[i]
+        return [
+            remote(o_f.at[:, at], fin_f.at[:, at], fin_s.at[0, i], fin_r.at[0, i], pair),
+            remote(o_b.at[:, at], fin_b.at[:, at], fin_s.at[1, i], fin_r.at[1, i], pair),
+        ]
+
     for i in range(CHUNKS):
         recv_all(y_b, h_b, back_sems, q_l, 2 * CHUNKS + i, parts[i])
     for i in range(CHUNKS):
         at = parts[i]
         recv_all(y_f, h_f, back_sems, q_l, i, at)
         recv_all(y_m, h_m, back_sems, q_l, CHUNKS + i, at)
-        mix = h_m[:, :, at].reshape(ROWS_MIX, step)
-        main = h_f[:, :, at].reshape(ROWS_MAIN, step)
-        moe_out[:, at] = (x_in[:, at].astype(F32) + dot(comb_f, main) + dot(cmix_f, mix)).astype(BF)
-        main = h_b[:, :, at].reshape(ROWS_MAIN, step)
-        input_grad[:, at] = (g_in[:, at].astype(F32) + dot(comb_b, main) + dot(cmix_b, mix)).astype(BF)
-
+        mix = h_m[:, :, at].reshape(ROWS_MIX, PARTS[i])
+        main = h_f[:, :, at].reshape(ROWS_MAIN, PARTS[i])
+        o_f[:, at] = (x_in[:, at].astype(F32) + dot(comb_f, main) + dot(cmix_f, mix)).astype(BF)
+        main = h_b[:, :, at].reshape(ROWS_MAIN, PARTS[i])
+        o_b[:, at] = (g_in[:, at].astype(F32) + dot(comb_b, main) + dot(cmix_b, mix)).astype(BF)
+        for copy in finished(i):
+            copy.start()
+    for i in range(CHUNKS):
+        at = parts[i]
+        for copy in finished(i):
+            copy.wait_recv()
+        moe_out[:, at] = fin_f[:, at]
+        input_grad[:, at] = fin_b[:, at]
+
+    for copy in tables:
+        copy.wait_send()
+    for i in range(CHUNKS):
+        for copy in finished(i):
+            copy.wait_send()
     for src, dst, b in ((s_f, r_f, 0), (s_b, r_b, 1), (s_m, r_m, 2)):
         sent_all(src, dst, out_sems, b, everything)
     for i in range(CHUNKS):
@@ -337,10 +369,14 @@
             pltpu.VMEM((GROUP, ROWS, wide), BF),
             pltpu.VMEM((GROUP, ROWS, wide), F32),
             pltpu.VMEM((GROUP, ROWS, hid), BF),
+            pltpu.VMEM((4, 2, tokens), jnp.int32),
+            pltpu.VMEM((tokens, width), BF), pltpu.VMEM((tokens, width), BF),
+            pltpu.VMEM((tokens, width), BF), pltpu.VMEM((tokens, width), BF),
             sems((2,)), sems((2,)), sems((4,)),
             sems((GROUP, 2 + CHUNKS)), sems((GROUP, 2 + CHUNKS)),
             sems((3, EXPERTS)), sems((3, EXPERTS)), sems((3,)),
             sems((3 * CHUNKS, EXPERTS)), sems((3 * CHUNKS, EXPERTS)), sems((3 * CHUNKS,)),
+            sems((2, CHUNKS)), sems((2, CHUNKS)), sems((4,)), sems((4,)),
         ],
         compiler_params=pltpu.CompilerParams(
             collective_id=0, has_side_effects=True, vmem_limit_bytes=60 * 1024 * 1024

time: 135 us -> 126 us (0.933)
  Pallas kernels: 134 us -> 125 us
    pallas_call x1, Pallas kernels: 132 us -> 123 us  [on_device(): pl.pallas_call(functools.partial(kernel, n_pipe), out_shape=(out, out), i...]
where the time goes in v3:
time: 126 us
  Pallas kernels  125 us (99%)
    pallas_call x1, Pallas kernels, on_device(): pl.pallas_call(functools.partial(kernel, n_pipe), out_shape=(out, out), i...  123 us

profile of v3, /device:TPU:1, one launch (start us, length us, event | category | flops | bytes accessed | tf_op | source)
XLA Modules:
  0.0 125.5 jit_solution(18219862856261446370)
XLA Ops:
  0.6 123.0 %shard_map.104 = (bf16[64,2560]{1,0:T(8,128)(2,1)}, bf16[64,2560]{1,0:T(8,128)(2,1)}) custom-call(bf16[64,2560]{1,0:T(8,128)(2,1)} %bitcast.24, bf16[64,2560]{1,0:T(8,128)(2,1)} %bitcast.25, s32[2,64]{1,0:T(2,128)} %bitcast.26, s32[2,64]{1,0:T(2,128)} %bitcast.27, s32[2,64]{1,0:T(2,128)} %bitcast.28, s32[2,64]{1,0:T(2,128)} %bitcast.29, ...), custom_call_target="tpu_custom_call" | custom-call | tf_op jit(solution)/shard_map/pallas_call | solution.py:352
  123.6 1.9 %shard_map.105 = (bf16[64,2560]{1,0:T(8,128)(2,1)}, bf16[64,2560]{1,0:T(8,128)(2,1)}) custom-call(bf16[64,2560]{1,0:T(8,128)(2,1)} %get-tuple-element.6.a, bf16[64,2560]{1,0:T(8,128)(2,1)} %get-tuple-element.7.b), custom_call_target="tpu_custom_call" | custom-call | tf_op jit(solution)/shard_map/pallas_call | solution.py:388

commit v4 on v3

--- a/solution.py
+++ b/solution.py
@@ -20,13 +20,14 @@
 PARTS = (768, 768, 640, 384)
 CHUNKS = len(PARTS)
 STEPS = 4
+FOLDS = 4
 
 
 def dot(a, b, ca=1, cb=0):
     return lax.dot_general(a, b, (((ca,), (cb,)), ((), ())), preferred_element_type=F32)
 
 
-def places(routes, gates, shift):
+def places(routes, gates):
     tokens = routes.shape[1]
     names = [routes[k : k + 1, :] for k in range(2)]
     experts = lax.broadcasted_iota(jnp.int32, (EXPERTS, tokens), 0)
@@ -34,15 +35,16 @@
     row = lax.broadcasted_iota(jnp.int32, (tokens, tokens), 0)
     column = lax.broadcasted_iota(jnp.int32, (tokens, tokens), 1)
     before = dot((onehot[0] + onehot[1]).astype(BF), (row < column).astype(BF))
-    sel = [jnp.zeros((rows, tokens), F32) for rows in (ROWS_MAIN, ROWS_MIX)]
+    sel = [jnp.zeros((rows, tokens), F32) for rows in (ROWS_MAIN, ROWS_MIX, ROWS_MIX)]
     at = [lax.broadcasted_iota(jnp.int32, s.shape, 0) for s in sel]
     comb = list(sel)
     for k in range(2):
         slot = jnp.sum(onehot[k] * before, axis=0, keepdims=True).astype(jnp.int32)
         gate = gates[k : k + 1, :].astype(F32) * (1.0 / 128.0)
         in_main = jnp.where(slot < MAIN, names[k] * MAIN + slot, -1)
-        in_mix = jnp.where(slot < MAIN, -1, names[k] * (2 * REST) + shift + slot - MAIN)
-        for i, place in enumerate((in_main, in_mix)):
+        in_low = jnp.where(slot < MAIN, -1, names[k] * (2 * REST) + slot - MAIN)
+        in_high = jnp.where(slot < MAIN, -1, in_low + REST)
+        for i, place in enumerate((in_main, in_low, in_high)):
             hit = (at[i] == place).astype(F32)
             sel[i] = sel[i] + hit
             comb[i] = comb[i] + hit * gate
@@ -55,10 +57,10 @@
     moe_out, input_grad,
     x_in, g_in, w_gu, w_d, raw, sv_out, sv,
     s_f, s_b, s_m, r_f, r_b, r_m,
-    y_f, y_b, y_m, h_f, h_b, h_m,
+    y_f, y_b, y_m, h_f, h_b, e_f, e_b, k_f, k_b,
     x_f, x_b, pre_b, proj_f, hid_f,
     meta, o_f, o_b, fin_f, fin_b,
-    pipe_s, pipe_r, loc, plane_s, plane_r, z_s, z_r, z_l, q_s, q_r, q_l, fin_s, fin_r, meta_s, meta_r,
+    pipe_s, pipe_r, loc, plane_s, plane_r, z_s, z_r, z_l, q_s, q_r, q_l, fin_s, fin_r, fin_l, meta_s, meta_r,
 ):
     width = acts.shape[1]
     hid = down.shape[0]
@@ -135,10 +137,9 @@
     row = lax.broadcasted_iota(jnp.int32, (ROWS, flat.shape[0]), 0)
     column = lax.broadcasted_iota(jnp.int32, (ROWS, flat.shape[0]), 1)
     late = row - ROWS_MAIN
-    slot = jnp.where(late < 0, row & (MAIN - 1), MAIN - REST + (late & (2 * REST - 1)))
+    slot = jnp.where(late < 0, row & (MAIN - 1), MAIN + (late & (REST - 1)))
     plane = jnp.where(late < 0, row >> 4, late >> 3)
-    known = (late < 0) | (slot >= MAIN)
-    base = jnp.where(known, slot * raw.shape[1] + plane * GROUP, -GROUP)
+    base = slot * raw.shape[1] + plane * GROUP
     for number in range(GROUP):
         pick = (column == base + number).astype(BF)
         sv_out[number] = dot(pick, flat).astype(BF)
@@ -152,8 +153,8 @@
 
     for copy in tables:
         copy.wait_recv()
-    sel_f, mix_f, comb_f, cmix_f = places(meta[0], meta[1], 0)
-    sel_b, mix_b, comb_b, cmix_b = places(meta[2], meta[3], REST)
+    sel_f, mix_f, _, comb_f, *rest_f = places(meta[0], meta[1])
+    sel_b, _, mix_b, comb_b, *rest_b = places(meta[2], meta[3])
 
     def columns(i):
         return pl.ds(pl.multiple_of(i * step, step), step)
@@ -224,8 +225,11 @@
     x_b[:ROWS_MAIN, :] = r_b[...].reshape(ROWS_MAIN, width)
     recv_all(s_m, r_m, out_sems, z_l, 2, everything)
     mixed = r_m[...].reshape(ROWS_MIX, width)
-    x_f[ROWS_MAIN:, :] = mixed
-    x_b[ROWS_MAIN:, :] = mixed
+    row = lax.broadcasted_iota(jnp.int32, (ROWS_MIX, ROWS_MIX), 0)
+    column = lax.broadcasted_iota(jnp.int32, (ROWS_MIX, ROWS_MIX), 1)
+    low = (row >> 3) * (2 * REST) + (row & (REST - 1))
+    x_b[ROWS_MAIN:, :] = dot((column == low + REST).astype(BF), mixed).astype(BF)
+    x_f[ROWS_MAIN:, :] = dot((column == low).astype(BF), mixed).astype(BF)
     for r in range(GROUP):
         if r in (1, 3):
             downs[r].wait_recv()
@@ -253,6 +257,14 @@
         y_m[:, :, at] = total[ROWS_MAIN:].astype(BF).reshape(EXPERTS, 2 * REST, PARTS[i])
         start_all(y_b, h_b, back_sems, q_l, 2 * CHUNKS + i, at)
 
+    def fold(dst, start, size):
+        shape = (ROWS_MIX, size)
+        upper = (lax.broadcasted_iota(jnp.int32, shape, 0) & (2 * REST - 1)) < REST
+        left = y_m[:, :, pl.ds(start, size)].reshape(shape).astype(F32)
+        right = y_m[:, :, pl.ds(width // 2 + start, size)].reshape(shape).astype(F32)
+        both = jnp.where(upper, left, right)
+        dst[:, :, pl.ds(start, size)] = both.reshape(EXPERTS, 2 * REST, size).astype(BF)
+
     def project(i):
         at = parts[i]
         for r in range(GROUP):
@@ -261,6 +273,9 @@
 
     for i in range(CHUNKS):
         backward(i)
+        if i == CHUNKS - 1:
+            fold(e_b, 0, width // 2)
+            start_all(e_b, k_b, back_sems, q_l, FOLDS, pl.ds(0, width // 2))
         if i == 1:
             recv_all(s_f, r_f, out_sems, z_l, 0, everything)
             x_f[:ROWS_MAIN, :] = r_f[...].reshape(ROWS_MAIN, width)
@@ -270,57 +285,75 @@
     for r in range(GROUP):
         a, b = proj_f[r, :, :hid], proj_f[r, :, hid:]
         hid_f[r] = (a * (1.0 / (1.0 + jnp.exp(-a))) * b).astype(BF)
-    for i in range(CHUNKS):
-        at = parts[i]
-        shape = (ROWS_MIX, PARTS[i])
+    quarter = width // STEPS
+    slabs = [pl.ds(i * quarter, quarter) for i in range(STEPS)]
+    for i in range(STEPS):
+        at = slabs[i]
         total = dot(hid_f[0], w_d[0, :, at])
         for r in range(1, GROUP):
             total = total + dot(hid_f[r], w_d[r, :, at])
-        y_f[:, :, at] = total[:ROWS_MAIN].astype(BF).reshape(EXPERTS, MAIN, PARTS[i])
-        from_forward = (lax.broadcasted_iota(jnp.int32, shape, 0) & (2 * REST - 1)) < REST
-        other = y_m[:, :, at].reshape(shape).astype(F32)
-        both = jnp.where(from_forward, total[ROWS_MAIN:], other)
-        y_m[:, :, at] = both.reshape(EXPERTS, 2 * REST, PARTS[i]).astype(BF)
+        y_f[:, :, at] = total[:ROWS_MAIN].astype(BF).reshape(EXPERTS, MAIN, quarter)
+        y_m[:, :, at] = total[ROWS_MAIN:].astype(BF).reshape(EXPERTS, 2 * REST, quarter)
         start_all(y_f, h_f, back_sems, q_l, i, at)
-        start_all(y_m, h_m, back_sems, q_l, CHUNKS + i, at)
-
-    def finished(i):
-        at = parts[i]
-        return [
-            remote(o_f.at[:, at], fin_f.at[:, at], fin_s.at[0, i], fin_r.at[0, i], pair),
-            remote(o_b.at[:, at], fin_b.at[:, at], fin_s.at[1, i], fin_r.at[1, i], pair),
-        ]
+        if i >= 2:
+            fold(e_f, (i - 2) * quarter, quarter)
+            start_all(e_f, k_f, back_sems, q_l, FOLDS + i - 1, slabs[i - 2])
+
+    def finished(which, i):
+        src, dst = ((o_f, fin_f), (o_b, fin_b))[which]
+        return remote(src.at[:, slabs[i]], dst.at[:, slabs[i]], fin_s.at[which, i], fin_r.at[which, i], pair)
+
+    def finish(which, i):
+        at = slabs[i]
+        own_in, main, further, comb, rest, out = (
+            (x_in, h_f, k_f, comb_f, rest_f, o_f),
+            (g_in, h_b, k_b, comb_b, rest_b, o_b),
+        )[which]
+        total = own_in[:, at].astype(F32) + dot(comb, main[:, :, at].reshape(ROWS_MAIN, quarter))
+        total = total + dot(rest[i // 2], further[:, :, slabs[i % 2]].reshape(ROWS_MIX, quarter))
+        out[:, at] = total.astype(BF)
+        finished(which, i).start()
+
+    def leave(which, i):
+        src, dst = ((fin_f, moe_out), (fin_b, input_grad))[which]
+        return pltpu.make_async_copy(src.at[:, slabs[i]], dst.at[:, slabs[i]], fin_l.at[which, i])
 
     for i in range(CHUNKS):
         recv_all(y_b, h_b, back_sems, q_l, 2 * CHUNKS + i, parts[i])
-    for i in range(CHUNKS):
-        at = parts[i]
-        recv_all(y_f, h_f, back_sems, q_l, i, at)
-        recv_all(y_m, h_m, back_sems, q_l, CHUNKS + i, at)
-        mix = h_m[:, :, at].reshape(ROWS_MIX, PARTS[i])
-        main = h_f[:, :, at].reshape(ROWS_MAIN, PARTS[i])
-        o_f[:, at] = (x_in[:, at].astype(F32) + dot(comb_f, main) + dot(cmix_f, mix)).astype(BF)
-        main = h_b[:, :, at].reshape(ROWS_MAIN, PARTS[i])
-        o_b[:, at] = (g_in[:, at].astype(F32) + dot(comb_b, main) + dot(cmix_b, mix)).astype(BF)
-        for copy in finished(i):
-            copy.start()
-    for i in range(CHUNKS):
-        at = parts[i]
-        for copy in finished(i):
-            copy.wait_recv()
-        moe_out[:, at] = fin_f[:, at]
-        input_grad[:, at] = fin_b[:, at]
+    recv_all(e_b, k_b, back_sems, q_l, FOLDS, pl.ds(0, width // 2))
+    for i in range(STEPS):
+        finish(1, i)
+    for i in range(STEPS):
+        finished(1, i).wait_recv()
+        leave(1, i).start()
+    for i in (0, 2, 1, 3):
+        if i == 0:
+            for k in range(3):
+                recv_all(y_f, h_f, back_sems, q_l, k, slabs[k])
+            recv_all(e_f, k_f, back_sems, q_l, FOLDS + 1, slabs[0])
+        if i == 1:
+            recv_all(y_f, h_f, back_sems, q_l, 3, slabs[3])
+            recv_all(e_f, k_f, back_sems, q_l, FOLDS + 2, slabs[1])
+        finish(0, i)
+    for i in (0, 2, 1, 3):
+        finished(0, i).wait_recv()
+        leave(0, i).start()
 
     for copy in tables:
         copy.wait_send()
-    for i in range(CHUNKS):
-        for copy in finished(i):
-            copy.wait_send()
+    for i in range(STEPS):
+        for which in (0, 1):
+            finished(which, i).wait_send()
+            leave(which, i).wait()
     for src, dst, b in ((s_f, r_f, 0), (s_b, r_b, 1), (s_m, r_m, 2)):
         sent_all(src, dst, out_sems, b, everything)
     for i in range(CHUNKS):
-        for src, dst, b in ((y_f, h_f, 0), (y_m, h_m, 1), (y_b, h_b, 2)):
-            sent_all(src, dst, back_sems, b * CHUNKS + i, parts[i])
+        sent_all(y_b, h_b, back_sems, 2 * CHUNKS + i, parts[i])
+    for i in range(STEPS):
+        sent_all(y_f, h_f, back_sems, i, slabs[i])
+    sent_all(e_b, k_b, back_sems, FOLDS, pl.ds(0, width // 2))
+    for i in range(2):
+        sent_all(e_f, k_f, back_sems, FOLDS + 1 + i, slabs[i])
     shift_f.wait_send()
     shift_b.wait_send()
     for r in (1, 2, 3):
@@ -346,6 +379,7 @@
     hbm = pl.BlockSpec(memory_space=pl.ANY)
     block = pltpu.VMEM((EXPERTS, MAIN, width), BF)
     mixed = pltpu.VMEM((EXPERTS, 2 * REST, width), BF)
+    folded = pltpu.VMEM((EXPERTS, 2 * REST, width // 2), BF)
     sems = pltpu.SemaphoreType.DMA
     out = jax.ShapeDtypeStruct((tokens, width), BF)
     by_slot = saved[0, 0].transpose(1, 0, 2)
@@ -353,7 +387,7 @@
         functools.partial(kernel, n_pipe),
         out_shape=(out, out),
         in_specs=[hbm, hbm, vmem, vmem, vmem, vmem, hbm, hbm, hbm],
-        out_specs=(vmem, vmem),
+        out_specs=(hbm, hbm),
         scratch_shapes=[
             pltpu.VMEM((tokens, width), BF),
             pltpu.VMEM((tokens, width), BF),
@@ -363,7 +397,7 @@
             pltpu.VMEM((GROUP, ROWS, wide), BF),
             pltpu.VMEM((GROUP, ROWS, wide), BF),
             block, block, mixed, block, block, mixed,
-            block, block, mixed, block, block, mixed,
+            block, block, mixed, block, block, folded, folded, folded, folded,
             pltpu.VMEM((ROWS, width), BF),
             pltpu.VMEM((ROWS, width), BF),
             pltpu.VMEM((GROUP, ROWS, wide), BF),
@@ -376,7 +410,7 @@
             sems((GROUP, 2 + CHUNKS)), sems((GROUP, 2 + CHUNKS)),
             sems((3, EXPERTS)), sems((3, EXPERTS)), sems((3,)),
             sems((3 * CHUNKS, EXPERTS)), sems((3 * CHUNKS, EXPERTS)), sems((3 * CHUNKS,)),
-            sems((2, CHUNKS)), sems((2, CHUNKS)), sems((4,)), sems((4,)),
+            sems((2, STEPS)), sems((2, STEPS)), sems((2, STEPS)), sems((4,)), sems((4,)),
         ],
         compiler_params=pltpu.CompilerParams(
             collective_id=0, has_side_effects=True, vmem_limit_bytes=60 * 1024 * 1024

time: 126 us -> 126 us (level)
  no operation moved by 1% of the time
where the time goes in v4:
time: 126 us; the launch traced here: 125 us
  Pallas kernels  125 us (99%)
    pallas_call x1, Pallas kernels, on_device(): pl.pallas_call(functools.partial(kernel, n_pipe), out_shape=(out, out), i...  123 us

profile of v4, /device:TPU:1, one launch (start us, length us, event | category | flops | bytes accessed | tf_op | source)
XLA Modules:
  0.0 125.4 jit_solution(4076716578642332134)
XLA Ops:
  0.6 122.9 %shard_map.104 = (bf16[64,2560]{1,0:T(8,128)(2,1)}, bf16[64,2560]{1,0:T(8,128)(2,1)}) custom-call(bf16[64,2560]{1,0:T(8,128)(2,1)} %bitcast.24, bf16[64,2560]{1,0:T(8,128)(2,1)} %bitcast.25, s32[2,64]{1,0:T(2,128)} %bitcast.26, s32[2,64]{1,0:T(2,128)} %bitcast.27, s32[2,64]{1,0:T(2,128)} %bitcast.28, s32[2,64]{1,0:T(2,128)} %bitcast.29, ...), custom_call_target="tpu_custom_call" | custom-call | tf_op jit(solution)/shard_map/pallas_call | solution.py:386
  123.5 1.9 %shard_map.105 = (bf16[64,2560]{1,0:T(8,128)(2,1)}, bf16[64,2560]{1,0:T(8,128)(2,1)}) custom-call(bf16[64,2560]{1,0:T(8,128)(2,1)} %get-tuple-element.6.a, bf16[64,2560]{1,0:T(8,128)(2,1)} %get-tuple-element.7.b), custom_call_target="tpu_custom_call" | custom-call | tf_op jit(solution)/shard_map/pallas_call | solution.py:422

commit v5 on v4

--- a/solution.py
+++ b/solution.py
@@ -17,7 +17,7 @@
 ROWS_MAIN = EXPERTS * MAIN
 ROWS_MIX = EXPERTS * 2 * REST
 ROWS = ROWS_MAIN + ROWS_MIX
-PARTS = (768, 768, 640, 384)
+PARTS = (896, 896, 512, 256)
 CHUNKS = len(PARTS)
 STEPS = 4
 FOLDS = 4
@@ -100,15 +100,19 @@
             src_ref=src, dst_ref=dst, send_sem=ssem, recv_sem=rsem, device_id=to, device_id_type=MESH
         )
 
-    shift_f = remote(acts, x_in, pipe_s.at[0], pipe_r.at[0], nxt)
-    shift_b = remote(grads, g_in, pipe_s.at[1], pipe_r.at[1], prv)
+    slabs = [pl.ds(i * step, step) for i in range(STEPS)]
+    shift_f = remote(acts, x_in, pipe_s.at[STEPS], pipe_r.at[STEPS], nxt)
+    shift_b = [
+        remote(grads.at[:, slabs[i]], g_in.at[:, slabs[i]], pipe_s.at[i], pipe_r.at[i], prv) for i in range(STEPS)
+    ]
     tables = [
         remote(table, meta.at[k], meta_s.at[k], meta_r.at[k], pair)
         for k, table in enumerate((routes_f, gate_f, routes_b, gate_b))
     ]
     for copy in tables:
         copy.start()
-    shift_b.start()
+    for copy in shift_b:
+        copy.start()
     shift_f.start()
 
     parts = [pl.ds(sum(PARTS[:i]), PARTS[i]) for i in range(CHUNKS)]
@@ -131,6 +135,67 @@
     kept = {r: saved_to(r) for r in (1, 2, 3)}
     downs[2].start()
     downs[1].start()
+
+    for copy in tables:
+        copy.wait_recv()
+    sel_f, mix_f, _, comb_f, *rest_f = places(meta[0], meta[1])
+    sel_b, _, mix_b, comb_b, *rest_b = places(meta[2], meta[3])
+
+    def columns(i):
+        return pl.ds(pl.multiple_of(i * step, step), step)
+
+    everything = pl.ds(0, width)
+
+    def travel(src, dst, sems, b, d, at):
+        ssem, rsem = sems
+        there = along(d)
+        return remote(
+            src.at[there, :, at], dst.at[z, :, at], ssem.at[b, d], rsem.at[b, d], {"expert": there * GROUP + line}
+        )
+
+    def arrive(src, dst, sems, b, d, at):
+        ssem, rsem = sems
+        there = along(EXPERTS - d)
+        return remote(
+            src.at[there, :, at], dst.at[there, :, at], ssem.at[b, d], rsem.at[b, d], {"expert": there * GROUP + line}
+        )
+
+    def start_all(src, dst, sems, local_sem, b, at):
+        for d in order:
+            travel(src, dst, sems, b, d, at).start()
+        pltpu.make_async_copy(src.at[z, :, at], dst.at[z, :, at], local_sem.at[b]).start()
+
+    def recv_all(src, dst, sems, local_sem, b, at):
+        for d in order[::-1]:
+            arrive(src, dst, sems, b, d, at).wait_recv()
+        pltpu.make_async_copy(src.at[z, :, at], dst.at[z, :, at], local_sem.at[b]).wait()
+
+    def sent_all(src, dst, sems, b, at):
+        for d in order:
+            travel(src, dst, sems, b, d, at).wait_send()
+
+    out_sems, back_sems = (z_s, z_r), (q_s, q_r)
+
+    for i, at in enumerate(slabs):
+        shift_b[i].wait_recv()
+        s_b[:, :, at] = dot(sel_b, g_in[:, at]).astype(BF).reshape(EXPERTS, MAIN, step)
+        start_all(s_b, r_b, out_sems, z_l, 2 + i, at)
+    shift_f.wait_recv()
+
+    @pl.loop(0, STEPS)
+    def _(i):
+        at = columns(i)
+        both = dot(mix_f, x_in[:, at]) + dot(mix_b, g_in[:, at])
+        s_m[:, :, at] = both.reshape(EXPERTS, 2 * REST, step).astype(BF)
+
+    start_all(s_m, r_m, out_sems, z_l, 1, everything)
+
+    @pl.loop(0, STEPS)
+    def _(i):
+        at = columns(i)
+        s_f[:, :, at] = dot(sel_f, x_in[:, at]).astype(BF).reshape(EXPERTS, MAIN, step)
+
+    start_all(s_f, r_f, out_sems, z_l, 0, everything)
 
     load_raw.wait()
     flat = raw[...].reshape(raw.shape[0] * raw.shape[1], raw.shape[2])
@@ -151,79 +216,15 @@
         gus[2][i].start()
         gus[1][i].start()
 
-    for copy in tables:
-        copy.wait_recv()
-    sel_f, mix_f, _, comb_f, *rest_f = places(meta[0], meta[1])
-    sel_b, _, mix_b, comb_b, *rest_b = places(meta[2], meta[3])
-
-    def columns(i):
-        return pl.ds(pl.multiple_of(i * step, step), step)
-
-    everything = pl.ds(0, width)
-
-    def travel(src, dst, sems, b, d, at):
-        ssem, rsem = sems
-        there = along(d)
-        return remote(
-            src.at[there, :, at], dst.at[z, :, at], ssem.at[b, d], rsem.at[b, d], {"expert": there * GROUP + line}
-        )
-
-    def arrive(src, dst, sems, b, d, at):
-        ssem, rsem = sems
-        there = along(EXPERTS - d)
-        return remote(
-            src.at[there, :, at], dst.at[there, :, at], ssem.at[b, d], rsem.at[b, d], {"expert": there * GROUP + line}
-        )
-
-    def start_all(src, dst, sems, local_sem, b, at):
-        for d in order:
-            travel(src, dst, sems, b, d, at).start()
-        pltpu.make_async_copy(src.at[z, :, at], dst.at[z, :, at], local_sem.at[b]).start()
-
-    def recv_all(src, dst, sems, local_sem, b, at):
-        for d in order[::-1]:
-            arrive(src, dst, sems, b, d, at).wait_recv()
-        pltpu.make_async_copy(src.at[z, :, at], dst.at[z, :, at], local_sem.at[b]).wait()
-
-    def sent_all(src, dst, sems, b, at):
-        for d in order:
-            travel(src, dst, sems, b, d, at).wait_send()
-
-    out_sems, back_sems = (z_s, z_r), (q_s, q_r)
-
-    shift_b.wait_recv()
-
-    @pl.loop(0, STEPS)
-    def _(i):
-        at = columns(i)
-        s_b[:, :, at] = dot(sel_b, g_in[:, at]).astype(BF).reshape(EXPERTS, MAIN, step)
-
-    start_all(s_b, r_b, out_sems, z_l, 1, everything)
-    shift_f.wait_recv()
-
-    @pl.loop(0, STEPS)
-    def _(i):
-        at = columns(i)
-        both = dot(mix_f, x_in[:, at]) + dot(mix_b, g_in[:, at])
-        s_m[:, :, at] = both.reshape(EXPERTS, 2 * REST, step).astype(BF)
-
-    start_all(s_m, r_m, out_sems, z_l, 2, everything)
-
-    @pl.loop(0, STEPS)
-    def _(i):
-        at = columns(i)
-        s_f[:, :, at] = dot(sel_f, x_in[:, at]).astype(BF).reshape(EXPERTS, MAIN, step)
-
-    start_all(s_f, r_f, out_sems, z_l, 0, everything)
-
     for copy in own:
         copy.wait()
     keep_own.wait()
     downs[2].wait_recv()
     downs[3].start()
-    recv_all(s_b, r_b, out_sems, z_l, 1, everything)
+    for i, at in enumerate(slabs):
+        recv_all(s_b, r_b, out_sems, z_l, 2 + i, at)
     x_b[:ROWS_MAIN, :] = r_b[...].reshape(ROWS_MAIN, width)
-    recv_all(s_m, r_m, out_sems, z_l, 2, everything)
+    recv_all(s_m, r_m, out_sems, z_l, 1, everything)
     mixed = r_m[...].reshape(ROWS_MIX, width)
     row = lax.broadcasted_iota(jnp.int32, (ROWS_MIX, ROWS_MIX), 0)
     column = lax.broadcasted_iota(jnp.int32, (ROWS_MIX, ROWS_MIX), 1)
@@ -265,6 +266,9 @@
         both = jnp.where(upper, left, right)
         dst[:, :, pl.ds(start, size)] = both.reshape(EXPERTS, 2 * REST, size).astype(BF)
 
+    last = PARTS[-1]
+    folds = ((0, width // 2 - last), (width // 2 - last, last))
+
     def project(i):
         at = parts[i]
         for r in range(GROUP):
@@ -273,9 +277,10 @@
 
     for i in range(CHUNKS):
         backward(i)
-        if i == CHUNKS - 1:
-            fold(e_b, 0, width // 2)
-            start_all(e_b, k_b, back_sems, q_l, FOLDS, pl.ds(0, width // 2))
+        if i >= CHUNKS - 2:
+            start, size = folds[i - CHUNKS + 2]
+            fold(e_b, start, size)
+            start_all(e_b, k_b, back_sems, q_l, FOLDS + 3 * (i - CHUNKS + 2), pl.ds(start, size))
         if i == 1:
             recv_all(s_f, r_f, out_sems, z_l, 0, everything)
             x_f[:ROWS_MAIN, :] = r_f[...].reshape(ROWS_MAIN, width)
@@ -285,18 +290,16 @@
     for r in range(GROUP):
         a, b = proj_f[r, :, :hid], proj_f[r, :, hid:]
         hid_f[r] = (a * (1.0 / (1.0 + jnp.exp(-a))) * b).astype(BF)
-    quarter = width // STEPS
-    slabs = [pl.ds(i * quarter, quarter) for i in range(STEPS)]
     for i in range(STEPS):
         at = slabs[i]
         total = dot(hid_f[0], w_d[0, :, at])
         for r in range(1, GROUP):
             total = total + dot(hid_f[r], w_d[r, :, at])
-        y_f[:, :, at] = total[:ROWS_MAIN].astype(BF).reshape(EXPERTS, MAIN, quarter)
-        y_m[:, :, at] = total[ROWS_MAIN:].astype(BF).reshape(EXPERTS, 2 * REST, quarter)
+        y_f[:, :, at] = total[:ROWS_MAIN].astype(BF).reshape(EXPERTS, MAIN, step)
+        y_m[:, :, at] = total[ROWS_MAIN:].astype(BF).reshape(EXPERTS, 2 * REST, step)
         start_all(y_f, h_f, back_sems, q_l, i, at)
         if i >= 2:
-            fold(e_f, (i - 2) * quarter, quarter)
+            fold(e_f, (i - 2) * step, step)
             start_all(e_f, k_f, back_sems, q_l, FOLDS + i - 1, slabs[i - 2])
 
     def finished(which, i):
@@ -309,8 +312,8 @@
             (x_in, h_f, k_f, comb_f, rest_f, o_f),
             (g_in, h_b, k_b, comb_b, rest_b, o_b),
         )[which]
-        total = own_in[:, at].astype(F32) + dot(comb, main[:, :, at].reshape(ROWS_MAIN, quarter))
-        total = total + dot(rest[i // 2], further[:, :, slabs[i % 2]].reshape(ROWS_MIX, quarter))
+        total = own_in[:, at].astype(F32) + dot(comb, main[:, :, at].reshape(ROWS_MAIN, step))
+        total = total + dot(rest[i // 2], further[:, :, slabs[i % 2]].reshape(ROWS_MIX, step))
         out[:, at] = total.astype(BF)
         finished(which, i).start()
 
@@ -320,7 +323,8 @@
 
     for i in range(CHUNKS):
         recv_all(y_b, h_b, back_sems, q_l, 2 * CHUNKS + i, parts[i])
-    recv_all(e_b, k_b, back_sems, q_l, FOLDS, pl.ds(0, width // 2))
+    for i in range(2):
+        recv_all(e_b, k_b, back_sems, q_l, FOLDS + 3 * i, pl.ds(*folds[i]))
     for i in range(STEPS):
         finish(1, i)
     for i in range(STEPS):
@@ -345,17 +349,20 @@
         for which in (0, 1):
             finished(which, i).wait_send()
             leave(which, i).wait()
-    for src, dst, b in ((s_f, r_f, 0), (s_b, r_b, 1), (s_m, r_m, 2)):
+    for src, dst, b in ((s_f, r_f, 0), (s_m, r_m, 1)):
         sent_all(src, dst, out_sems, b, everything)
+    for i, at in enumerate(slabs):
+        sent_all(s_b, r_b, out_sems, 2 + i, at)
     for i in range(CHUNKS):
         sent_all(y_b, h_b, back_sems, 2 * CHUNKS + i, parts[i])
     for i in range(STEPS):
         sent_all(y_f, h_f, back_sems, i, slabs[i])
-    sent_all(e_b, k_b, back_sems, FOLDS, pl.ds(0, width // 2))
     for i in range(2):
         sent_all(e_f, k_f, back_sems, FOLDS + 1 + i, slabs[i])
+        sent_all(e_b, k_b, back_sems, FOLDS + 3 * i, pl.ds(*folds[i]))
     shift_f.wait_send()
-    shift_b.wait_send()
+    for copy in shift_b:
+        copy.wait_send()
     for r in (1, 2, 3):
         downs[r].wait_send()
         kept[r].wait_send()
@@ -406,9 +413,9 @@
             pltpu.VMEM((4, 2, tokens), jnp.int32),
             pltpu.VMEM((tokens, width), BF), pltpu.VMEM((tokens, width), BF),
             pltpu.VMEM((tokens, width), BF), pltpu.VMEM((tokens, width), BF),
-            sems((2,)), sems((2,)), sems((4,)),
+            sems((STEPS + 1,)), sems((STEPS + 1,)), sems((4,)),
             sems((GROUP, 2 + CHUNKS)), sems((GROUP, 2 + CHUNKS)),
-            sems((3, EXPERTS)), sems((3, EXPERTS)), sems((3,)),
+            sems((2 + STEPS, EXPERTS)), sems((2 + STEPS, EXPERTS)), sems((2 + STEPS,)),
             sems((3 * CHUNKS, EXPERTS)), sems((3 * CHUNKS, EXPERTS)), sems((3 * CHUNKS,)),
             sems((2, STEPS)), sems((2, STEPS)), sems((2, STEPS)), sems((4,)), sems((4,)),
         ],

time: 126 us -> 125 us (level)
  no operation moved by 1% of the time
where the time goes in v5:
time: 125 us
  Pallas kernels  124 us (99%)
    pallas_call x1, Pallas kernels, on_device(): pl.pallas_call(functools.partial(kernel, n_pipe), out_shape=(out, out), i...  122 us

profile of v5, /device:TPU:1, one launch (start us, length us, event | category | flops | bytes accessed | tf_op | source)
XLA Modules:
  0.0 124.8 jit_solution(11180784067098919159)
XLA Ops:
  0.6 122.2 %shard_map.104 = (bf16[64,2560]{1,0:T(8,128)(2,1)}, bf16[64,2560]{1,0:T(8,128)(2,1)}) custom-call(bf16[64,2560]{1,0:T(8,128)(2,1)} %bitcast.24, bf16[64,2560]{1,0:T(8,128)(2,1)} %bitcast.25, s32[2,64]{1,0:T(2,128)} %bitcast.26, s32[2,64]{1,0:T(2,128)} %bitcast.27, s32[2,64]{1,0:T(2,128)} %bitcast.28, s32[2,64]{1,0:T(2,128)} %bitcast.29, ...), custom_call_target="tpu_custom_call" | custom-call | tf_op jit(solution)/shard_map/pallas_call | solution.py:393
  122.9 1.9 %shard_map.105 = (bf16[64,2560]{1,0:T(8,128)(2,1)}, bf16[64,2560]{1,0:T(8,128)(2,1)}) custom-call(bf16[64,2560]{1,0:T(8,128)(2,1)} %get-tuple-element.6.a, bf16[64,2560]{1,0:T(8,128)(2,1)} %get-tuple-element.7.b), custom_call_target="tpu_custom_call" | custom-call | tf_op jit(solution)/shard_map/pallas_call | solution.py:429
